TPU v7x, 32 devices: a whole 2x2x4 slice. The times are simulated.
32 devices in a mesh: samp: 8 (over y, x, core), cent: 4 (over z).
Axes of the slice: x: 2, y: 2, z: 4, core: 2. Of those that a mesh axis runs over, the one named last changes fastest.
Arguments:
- embeddings: float32 [16384, 1024], P(('samp', 'cent')), may hold values from -40 to 40
- assignment: int32 [16384], P(('samp', 'cent')), may hold values from 0 to 2047, as said below
- owner_map: int32 [2048], replicated, may hold values from 0 to 31, as said below
Outputs:
- centroid: float32 [2048, 1024], P(('samp', 'cent'))
- representative: float32 [2048, 1024], P(('samp', 'cent'))
- keep_weight: float32 [16384], P(('samp', 'cent'))
Inputs may be any that keep to these rules, and one draw needn't show every extreme that they name: `owner_map`: every device index, samp-major, owns exactly 64 clusters. `assignment`: of the 512 rows of one device, at most 64 lie in clusters owned by any one device; in every draw some device owns clusters that hold exactly 64 rows of every device.
All inputs are finite; a program needn't handle non-finite values.
Results may differ from a plain program's by a relative error of at most 0.0034.
Values may be sent and summed in bfloat16 or wider, within the bound.
A program may use at most 64 MiB of HBM per device.

v0:
```python
import jax
import jax.numpy as jnp
from jax import lax
from jax.sharding import PartitionSpec as P

EPSILON = 1e-06
SHARPNESS = 8.0


def all_pairs(arrived, arrived_tags, validity, block_size):
    slot_count, feature_width = arrived.shape
    block_count = slot_count // block_size

    def score_block(pieces):
        block_rows, block_tags = pieces
        gram = jnp.einsum("rd,qd->rq", block_rows, arrived, preferred_element_type=jnp.float32)
        same_cluster = (block_tags[:, None] == arrived_tags[None, :]) & validity[None, :]
        similar = jnp.sum(jnp.where(same_cluster, gram, 0.0), axis=1)
        density = jnp.sum(jnp.where(same_cluster, jnp.exp(SHARPNESS * (gram - 1.0)), 0.0), axis=1)
        return (similar, density)

    similar, density = lax.map(
        score_block,
        (
            arrived.reshape(block_count, block_size, feature_width),
            arrived_tags.reshape(block_count, block_size),
        ),
    )
    return (similar.reshape(slot_count), density.reshape(slot_count))


def on_device(embeddings, assignment, owner_map):
    row_count, feature_width = embeddings.shape
    n_samp = lax.axis_size("samp")
    n_cent = lax.axis_size("cent")
    devices = n_samp * n_cent
    clusters = owner_map.shape[0]
    per_owner = clusters // devices
    capacity = 4 * row_count // devices
    slot_count = devices * capacity
    unit_rows = (
        embeddings * lax.rsqrt(jnp.sum(embeddings * embeddings, axis=1, keepdims=True) + EPSILON)
    ).astype(jnp.bfloat16)
    destination = owner_map[assignment]
    cluster_order = jnp.argsort(owner_map, stable=True)
    position = (
        jnp.zeros((clusters,), jnp.int32)
        .at[cluster_order]
        .set(jnp.arange(clusters, dtype=jnp.int32))
    )
    local_rank = position[assignment] - destination * per_owner
    dest_onehot = (destination[:, None] == jnp.arange(devices, dtype=jnp.int32)[None, :]).astype(
        jnp.int32
    )
    within_rank = jnp.sum(jnp.cumsum(dest_onehot, axis=0) * dest_onehot, axis=1) - 1
    slot_index = destination * capacity + within_rank
    outgoing = jnp.zeros((slot_count, feature_width), jnp.bfloat16).at[slot_index].set(unit_rows)
    labels = (
        jnp.zeros((slot_count,), jnp.bfloat16)
        .at[slot_index]
        .set((local_rank + 1).astype(jnp.bfloat16))
    )
    arrived, arrived_labels = (
        lax.all_to_all(outgoing, ("samp", "cent"), split_axis=0, concat_axis=0, tiled=True),
        lax.all_to_all(labels, ("samp", "cent"), split_axis=0, concat_axis=0, tiled=True),
    )
    arrived_tags = arrived_labels.astype(jnp.int32) - 1
    validity = arrived_tags >= 0
    block_size = min(512, slot_count)
    similar, density = all_pairs(arrived, arrived_tags, validity, block_size)
    member = arrived_tags[None, :] == jnp.arange(per_owner, dtype=jnp.int32)[:, None]
    member_bf = member.astype(jnp.bfloat16)
    cluster_sums = jnp.dot(member_bf, arrived, preferred_element_type=jnp.float32)
    inverse_norm = lax.rsqrt(jnp.sum(cluster_sums * cluster_sums, axis=1) + EPSILON)
    row_scale = jnp.sum(member.astype(jnp.float32) * inverse_norm[:, None], axis=0)
    spread = 1.0 - similar * row_scale
    weight = jnp.where(validity, jnp.exp(spread) / jnp.where(validity, density, 1.0), 0.0)
    weighted = jnp.dot(
        member_bf * weight.astype(jnp.bfloat16)[None, :],
        arrived,
        preferred_element_type=jnp.float32,
    )
    centroid = cluster_sums * inverse_norm[:, None]
    representative = weighted * lax.rsqrt(
        jnp.sum(weighted * weighted, axis=1, keepdims=True) + EPSILON
    )
    returned = lax.all_to_all(weight, ("samp", "cent"), split_axis=0, concat_axis=0, tiled=True)
    keep_weight = returned[slot_index]
    return (centroid, representative, keep_weight)


def solution(mesh):
    in_specs = (P(("samp", "cent"), None), P(("samp", "cent")), P())
    out_specs = (P(("samp", "cent"), None), P(("samp", "cent"), None), P(("samp", "cent")))
    return jax.shard_map(
        on_device, mesh=mesh, in_specs=in_specs, out_specs=out_specs, check_vma=False
    )
```

profile of v0, /device:TPU:0, one launch (start us, length us, event | category | flops | bytes accessed | tf_op | source)
XLA Modules:
  0.0 188.5 jit_solution(18284801313536207739)
XLA Ops:
  0.6 5.9 %sort.17 = (s32[2048]{0:T(1024)}, s32[2048]{0:T(1024)S(1)}) sort(s32[2048]{0:T(1024)} %param.7, s32[2048]{0:T(1024)S(1)} %iota.19), dimensions={0}, to_apply=%region_3.4 | sort | flops 22528 | bytes 32768 | tf_op jit(solution)/shard_map/jit(argsort)/sort | solution.py:45
  7.2 3.4 %gather_fusion = s32[512]{0:T(512)S(1)} fusion(s32[2048]{0:T(1024)} %param.7, s32[1024]{0:T(1024)S(1)} %pad_clamp_fusion.1), kind=kCustom, calls=%fused_computation | custom fusion | bytes 6144 | tf_op jit(solution)/shard_map/gather | solution.py:44
  10.6 8.0 %scatter_custom_fusion = s32[2048]{0:T(1024)S(1)} fusion(s32[2048]{0:T(1024)S(1)} %compare_select_fusion.2, s32[2048]{0:T(1024)S(1)} %iota.20, s32[]{:T(128)} %constant.62.clone.1), kind=kCustom, calls=%fused_computation.51 | custom fusion | bytes 8196 | tf_op jit(solution)/shard_map/scatter | solution.py:49
  18.7 3.1 %gather_fusion.1 = s32[512]{0:T(512)S(1)} fusion(s32[2048]{0:T(1024)S(1)} %scatter_custom_fusion, s32[1024]{0:T(1024)S(1)} %pad_clamp_fusion.1), kind=kCustom, calls=%fused_computation.1 | custom fusion | bytes 6144 | tf_op jit(solution)/shard_map/gather | solution.py:51
  21.8 1.2 reduce-window.6
  23.4 3.8 %scatter_custom_fusion.1 = bf16[2048]{0:T(1024)(128)(2,1)S(1)} fusion(s32[512]{0:T(512)S(1)} %bitcast.58, bf16[512]{0:T(512)(128)(2,1)S(1)} %get-tuple-element.129, bf16[]{:T(256)} %constant.61.clone.1), kind=kCustom, calls=%fused_computation.56 | custom fusion | bytes 4098 | tf_op jit(solution)/shard_map/scatter | solution.py:61
  27.2 0.7 all_to_all.27
  27.9 7.3 %all-to-all-start = ((bf16[32,64,1]{1,2,0:T(2,128)(2,1)}), bf16[32,64,1]{1,2,0:T(2,128)(2,1)S(1)}, u32[]{:S(2)}, u32[]{:S(2)}) async-start(bf16[32,64,1]{1,2,0:T(2,128)(2,1)} %all_to_all.27), calls=%async_computation | async-start | bytes 32768 | tf_op jit(solution)/shard_map/all_to_all | solution.py:65
  35.4 5.3 %scatter_custom_fusion.2 = bf16[2048,1024]{1,0:T(8,128)(2,1)} fusion(s32[512]{0:T(512)S(1)} %bitcast.59, bf16[]{:T(256)} %constant.61.clone.1, f32[512,1024]{1,0:T(8,128)S(1)} %copy-done, f32[512]{0:T(512)S(1)} %add_rsqrt_fusion), kind=kCustom, calls=%fused_computation.16 | custom fusion | flops 1048576 | bytes 6293506 | tf_op jit(solution)/shard_map/scatter | solution.py:57
  40.8 1.6 all-to-all-done
  42.3 4.6 %all-to-all-start.1 = ((bf16[32,64,1024]{2,1,0:T(8,128)(2,1)}), bf16[32,64,1024]{2,1,0:T(8,128)(2,1)}, u32[]{:S(2)}, u32[]{:S(2)}) async-start(bf16[32,64,1024]{2,1,0:T(8,128)(2,1)} %bitcast.48), calls=%async_computation.1 | async-start | bytes 8388608 | tf_op jit(solution)/shard_map/all_to_all | solution.py:64
  47.2 91.8 %all-to-all-done.1 = bf16[32,64,1024]{2,1,0:T(8,128)(2,1)} async-done(((bf16[32,64,1024]{2,1,0:T(8,128)(2,1)}), bf16[32,64,1024]{2,1,0:T(8,128)(2,1)}, u32[]{:S(2)}, u32[]{:S(2)}) %all-to-all-start.1) | async-done | bytes 4194336 | tf_op jit(solution)/shard_map/all_to_all | solution.py:64
  138.9 3.1 %multiply_reduce_fusion.2 = (f32[64]{0:T(128)S(1)}, f32[64,1024]{1,0:T(8,128)S(1)}) fusion(bf16[2048,1024]{1,0:T(8,128)(2,1)} %bitcast.9, s32[2048]{0:T(1024)S(1)} %sub.41), kind=kOutput, calls=%fused_computation.25 | convolution fusion | flops 268697536 | bytes 4464896 | tf_op jit(solution)/shard_map/dot_general | solution.py:73
  142.1 23.8 %while.14 = (s32[]{:T(128)}, f32[4,512]{1,0:T(4,128)S(1)}, f32[4,512]{1,0:T(4,128)S(1)}, s32[4,512]{1,0:T(4,128)S(1)}, s32[2048]{0:T(1024)S(1)}, /*index=5*/pred...) while((s32[]{:T(128)}, f32[4,512]{1,0:T(4,128)S(1)}, ...), condition=%wide.region_12.13_spmd, body=%wide.region_9.12_spmd.sunk | while | flops 2155871232 | bytes 5271677 | solution.py:22
  142.1 5.8 %select_reduce_fusion.4 = (f32[512]{0:T(512)S(1)}, f32[512]{0:T(512)S(1)}) fusion(s32[2048]{0:T(1024)S(1)} %get-tuple-element.214, s32[512]{0:T(512)S(1)} %bitcast.52, pred[2048]{0:T(1024)(128)(4,1)S(1)} %get-tuple-element.215, bf16[2048,1024]{1,0:T(8,128)(2,1)} %get-tuple-element.217, bf16[4,512,1024]{2,1,0:T(8,128)(2,1)} %get-tuple-element.216, ...), kind=kOutput, calls=%fused_computation.6.clone.1 | convolution fusion | flops 2155871232 | bytes 5259268 | tf_op jit(solution)/shard_map/while/body/eval_jaxpr/rd,qd->rq/dot_general | solution.py:16
  148.0 5.8 %select_reduce_fusion.4 = (f32[512]{0:T(512)S(1)}, f32[512]{0:T(512)S(1)}) fusion(s32[2048]{0:T(1024)S(1)} %get-tuple-element.214, s32[512]{0:T(512)S(1)} %bitcast.52, pred[2048]{0:T(1024)(128)(4,1)S(1)} %get-tuple-element.215, bf16[2048,1024]{1,0:T(8,128)(2,1)} %get-tuple-element.217, bf16[4,512,1024]{2,1,0:T(8,128)(2,1)} %get-tuple-element.216, ...), kind=kOutput, calls=%fused_computation.6.clone.1 | convolution fusion | flops 2155871232 | bytes 5259268 | tf_op jit(solution)/shard_map/while/body/eval_jaxpr/rd,qd->rq/dot_general | solution.py:16
  154.0 5.8 %select_reduce_fusion.4 = (f32[512]{0:T(512)S(1)}, f32[512]{0:T(512)S(1)}) fusion(s32[2048]{0:T(1024)S(1)} %get-tuple-element.214, s32[512]{0:T(512)S(1)} %bitcast.52, pred[2048]{0:T(1024)(128)(4,1)S(1)} %get-tuple-element.215, bf16[2048,1024]{1,0:T(8,128)(2,1)} %get-tuple-element.217, bf16[4,512,1024]{2,1,0:T(8,128)(2,1)} %get-tuple-element.216, ...), kind=kOutput, calls=%fused_computation.6.clone.1 | convolution fusion | flops 2155871232 | bytes 5259268 | tf_op jit(solution)/shard_map/while/body/eval_jaxpr/rd,qd->rq/dot_general | solution.py:16
  159.9 5.8 %select_reduce_fusion.4 = (f32[512]{0:T(512)S(1)}, f32[512]{0:T(512)S(1)}) fusion(s32[2048]{0:T(1024)S(1)} %get-tuple-element.214, s32[512]{0:T(512)S(1)} %bitcast.52, pred[2048]{0:T(1024)(128)(4,1)S(1)} %get-tuple-element.215, bf16[2048,1024]{1,0:T(8,128)(2,1)} %get-tuple-element.217, bf16[4,512,1024]{2,1,0:T(8,128)(2,1)} %get-tuple-element.216, ...), kind=kOutput, calls=%fused_computation.6.clone.1 | convolution fusion | flops 2155871232 | bytes 5259268 | tf_op jit(solution)/shard_map/while/body/eval_jaxpr/rd,qd->rq/dot_general | solution.py:16
  166.3 3.1 %multiply_reduce_fusion.1 = (f32[64]{0:T(128)S(1)}, f32[64,1024]{1,0:T(8,128)S(1)}) fusion(bf16[2048,1024]{1,0:T(8,128)(2,1)} %bitcast.9, s32[2048]{0:T(1024)S(1)} %get-tuple-element.222, bf16[2048]{0:T(1024)(128)(2,1)S(1)} %select_convert_fusion), kind=kOutput, calls=%fused_computation.24 | convolution fusion | flops 268828608 | bytes 4468992 | tf_op jit(solution)/shard_map/dot_general | solution.py:78
  170.2 5.6 %all-to-all-start.2 = ((f32[32,64,1]{1,2,0:T(1,128)}), f32[32,64,1]{1,2,0:T(1,128)S(1)}, u32[]{:S(2)}, u32[]{:S(2)}) async-start(f32[32,64,1]{1,2,0:T(1,128)} %compare_select_fusion), calls=%async_computation.2 | async-start | bytes 32768 | tf_op jit(solution)/shard_map/all_to_all | solution.py:87
  175.7 0.9 broadcast_multiply_fusion
  176.6 6.3 %all-to-all-done.2 = f32[32,64,1]{1,2,0:T(1,128)S(1)} async-done(((f32[32,64,1]{1,2,0:T(1,128)}), f32[32,64,1]{1,2,0:T(1,128)S(1)}, u32[]{:S(2)}, u32[]{:S(2)}) %all-to-all-start.2) | async-done | bytes 8224 | tf_op jit(solution)/shard_map/all_to_all | solution.py:87
  183.4 0.7 reduce.11
  184.2 4.3 %gather_fusion.2 = f32[512]{0:T(512)} fusion(f32[2048]{0:T(1024)S(1)} %all_to_all.26, s32[1024]{0:T(1024)S(1)} %pad_clamp_fusion), kind=kCustom, calls=%fused_computation.2 | custom fusion | bytes 6144 | tf_op jit(solution)/shard_map/gather | solution.py:88
  (47 shorter events, 3.7 us)
Async XLA Ops:
  0.6 34.6 %copy-start = (f32[512,1024]{1,0:T(8,128)S(1)}, f32[512,1024]{1,0:T(8,128)}, u32[]{:S(2)}) copy-start(f32[512,1024]{1,0:T(8,128)} %param.5) | copy-start | bytes 6291460
  27.9 14.5 %all-to-all-start = ((bf16[32,64,1]{1,2,0:T(2,128)(2,1)}), bf16[32,64,1]{1,2,0:T(2,128)(2,1)S(1)}, u32[]{:S(2)}, u32[]{:S(2)}) async-start(bf16[32,64,1]{1,2,0:T(2,128)(2,1)} %all_to_all.27), calls=%async_computation | async-start | bytes 32768 | tf_op jit(solution)/shard_map/all_to_all | solution.py:65
  42.3 96.6 %all-to-all-start.1 = ((bf16[32,64,1024]{2,1,0:T(8,128)(2,1)}), bf16[32,64,1024]{2,1,0:T(8,128)(2,1)}, u32[]{:S(2)}, u32[]{:S(2)}) async-start(bf16[32,64,1024]{2,1,0:T(8,128)(2,1)} %bitcast.48), calls=%async_computation.1 | async-start | bytes 8388608 | tf_op jit(solution)/shard_map/all_to_all | solution.py:64
  170.2 12.8 %all-to-all-start.2 = ((f32[32,64,1]{1,2,0:T(1,128)}), f32[32,64,1]{1,2,0:T(1,128)S(1)}, u32[]{:S(2)}, u32[]{:S(2)}) async-start(f32[32,64,1]{1,2,0:T(1,128)} %compare_select_fusion), calls=%async_computation.2 | async-start | bytes 32768 | tf_op jit(solution)/shard_map/all_to_all | solution.py:87
where the time goes:
time: 189 us; the launch traced here: 188 us
  waiting for transfers between devices  99.6 us (53%)
  matrix products  29.5 us (16%)
  local copies, waits for them, and re-layouts  25 us (13%)
  starting transfers between devices  17.5 us (9%)
  other arithmetic  15.9 us (8%)
    all_to_all x1, waiting for transfers between devices, on_device(): lax.all_to_all(outgoing, ('samp', 'cent'), split_axis=0, concat_axis=0, t...  91.8 us
    dot_general x4, matrix products, score_block(): jnp.einsum('rd,qd->rq', block_rows, arrived, preferred_element_type=jnp.f...  23.2 us
    scatter x1, local copies, waits for them, and re-layouts, on_device(): position = jnp.zeros((clusters,), jnp.int32).at[cluster_order].set(jnp.ar...  8.05 us
    all_to_all x1, starting transfers between devices, on_device(): lax.all_to_all(labels, ('samp', 'cent'), split_axis=0, concat_axis=0, til...  7.33 us
    all_to_all x1, waiting for transfers between devices, on_device(): lax.all_to_all(weight, ('samp', 'cent'), split_axis=0, concat_axis=0, til...  6.3 us
    sort x1, other arithmetic, on_device(): cluster_order = jnp.argsort(owner_map, stable=True)  5.88 us
    all_to_all x1, starting transfers between devices, on_device(): lax.all_to_all(weight, ('samp', 'cent'), split_axis=0, concat_axis=0, til...  5.58 us
    scatter x1, other arithmetic, on_device(): jnp.zeros((slot_count, feature_width), jnp.bfloat16).at[slot_index]  5.32 us
  transfers between devices with their start and end apart: 3, of which 3 were waited for; matrix products, arithmetic and copies ran while one was open for 4% of the time, Pallas kernels for 0%

commit v1 on v0

--- a/solution.py
+++ b/solution.py
@@ -1,10 +1,250 @@
+import functools
+
 import jax
 import jax.numpy as jnp
 from jax import lax
+from jax.experimental import pallas as pl
+from jax.experimental.pallas import tpu as pltpu
 from jax.sharding import PartitionSpec as P
 
 EPSILON = 1e-06
 SHARPNESS = 8.0
+LANES = 128
+BF = jnp.bfloat16
+F32 = jnp.float32
+MESH = pl.DeviceIdType.MESH
+
+
+def iota(shape, axis):
+    return lax.broadcasted_iota(jnp.int32, shape, axis)
+
+
+def row_dot(a, b):
+    return lax.dot_general(a, b, (((1,), (1,)), ((), ())), preferred_element_type=F32)
+
+
+def pack_kernel(devices, near, pool, emb_ref, assign_ref, owner_ref, send_ref, pool_ref, lab_ref, meta_ref):
+    rows = emb_ref.shape[0]
+    clusters = owner_ref.shape[1]
+    upper = (iota((rows, rows), 0) < iota((rows, rows), 1)).astype(BF)
+    owner = owner_ref[...]
+    owner_hot = (iota((devices, clusters), 0) == owner).astype(F32)
+    base = jnp.zeros((devices, 1), F32)
+    ranks = []
+    for start in range(0, clusters, rows):
+        part = owner_hot[:, start:start + rows]
+        before = jnp.dot(part.astype(BF), upper, preferred_element_type=F32) + base
+        ranks.append(jnp.sum(part * before, axis=0, keepdims=True))
+        base = base + jnp.sum(part, axis=1, keepdims=True)
+    rank = jnp.concatenate(ranks, axis=1)
+    assign = assign_ref[...]
+    pick = (iota((clusters, rows), 0) == assign).astype(BF)
+    which = iota((8, clusters), 0)
+    table = jnp.where(which == 0, owner.astype(F32), jnp.where(which == 1, rank, 0.0)).astype(BF)
+    found = jnp.dot(table, pick, preferred_element_type=F32)
+    dest = found[0:1, :].astype(jnp.int32)
+    label = found[1:2, :] + 1.0
+    dest_hot = (iota((devices, rows), 0) == dest).astype(F32)
+    before = jnp.dot(dest_hot.astype(BF), upper, preferred_element_type=F32)
+    within = jnp.sum(dest_hot * before, axis=0, keepdims=True)
+    over = (within >= near).astype(F32)
+    over_before = jnp.dot(
+        jnp.broadcast_to(over, (8, rows)).astype(BF), upper, preferred_element_type=F32
+    )[0:1, :]
+    excess = jnp.sum(over, axis=1, keepdims=True) > pool
+    within = within.astype(jnp.int32)
+    is_over = over > 0.0
+    pool_at = over_before.astype(jnp.int32)
+    column = jnp.where(is_over, jnp.minimum(near + pool_at, LANES - 2), within)
+    col_hot = (iota((LANES, rows), 0) == column).astype(BF)
+    labels = row_dot((dest_hot * label).astype(BF), col_hot)
+    lane = iota((devices, LANES), 1)
+    lab_ref[:, 0, :] = jnp.where(lane == LANES - 1, excess.astype(F32), labels)
+    meta_ref[...] = jnp.where(iota((8, rows), 0) == 0, dest, column)
+    emb = emb_ref[...]
+    unit = (emb * lax.rsqrt(jnp.sum(emb * emb, axis=1, keepdims=True) + EPSILON)).astype(BF)
+    slot = jnp.where(is_over, -1, dest * near + within)
+    step = devices * near // 4
+    for start in range(0, devices * near, step):
+        hot = (iota((step, rows), 0) + start == slot).astype(BF)
+        out = jnp.dot(hot, unit, preferred_element_type=F32).astype(BF)
+        send_ref[start // near:(start + step) // near] = out.reshape(step // near, near, -1)
+    pool_hot = (iota((pool, rows), 0) == jnp.where(is_over, pool_at, -1)).astype(BF)
+    pool_ref[...] = jnp.dot(pool_hot, unit, preferred_element_type=F32).astype(BF)
+
+
+def who(n_cent, index):
+    return (index // n_cent, index % n_cent)
+
+
+def enter(n_samp, n_cent, me):
+    devices = n_samp * n_cent
+    barrier = pltpu.get_barrier_semaphore()
+
+    def greet(k, _):
+        pl.semaphore_signal(
+            barrier, inc=1, device_id=who(n_cent, (me + k) % devices), device_id_type=MESH
+        )
+        return 0
+
+    lax.fori_loop(1, devices, greet, 0)
+    pl.semaphore_wait(barrier, devices - 1)
+
+
+def exchange_kernel(
+    n_samp, n_cent, send_ref, pool_ref, lab_ref, recv_ref, pools_ref, labs_ref,
+    own_sem, row_out, row_in, lab_out, lab_in, near_out, near_in, far_out, far_in,
+):
+    devices = n_samp * n_cent
+    samp = lax.axis_index("samp")
+    cent = lax.axis_index("cent")
+    me = samp * n_cent + cent
+    own = [
+        pltpu.make_async_copy(send_ref.at[me], recv_ref.at[me], own_sem.at[0]),
+        pltpu.make_async_copy(lab_ref.at[me], labs_ref.at[me], own_sem.at[1]),
+        pltpu.make_async_copy(pool_ref, pools_ref.at[samp, cent], own_sem.at[2]),
+    ]
+    for copy in own:
+        copy.start()
+    enter(n_samp, n_cent, me)
+
+    def near_copy(k, slot):
+        return pltpu.make_async_remote_copy(
+            pool_ref, pools_ref.at[samp, slot], near_out.at[k], near_in.at[slot],
+            device_id=(samp, (cent + k) % n_cent), device_id_type=MESH,
+        )
+
+    def lab_copy(k, slot):
+        peer = (me + k) % devices
+        return pltpu.make_async_remote_copy(
+            lab_ref.at[peer], labs_ref.at[slot], lab_out.at[k], lab_in.at[slot],
+            device_id=who(n_cent, peer), device_id_type=MESH,
+        )
+
+    def row_copy(k, slot):
+        peer = (me + k) % devices
+        return pltpu.make_async_remote_copy(
+            send_ref.at[peer], recv_ref.at[slot], row_out.at[k], row_in.at[slot],
+            device_id=who(n_cent, peer), device_id_type=MESH,
+        )
+
+    def far_copy(k, slot):
+        return pltpu.make_async_remote_copy(
+            pools_ref.at[samp], pools_ref.at[slot], far_out.at[k], far_in.at[slot],
+            device_id=((samp + k) % n_samp, cent), device_id_type=MESH,
+        )
+
+    def loop(count, body):
+        def step(k, _):
+            body(k)
+            return 0
+        lax.fori_loop(1, count, step, 0)
+
+    loop(n_cent, lambda k: near_copy(k, cent).start())
+    loop(devices, lambda k: row_copy(k, me).start())
+    loop(devices, lambda k: lab_copy(k, me).start())
+    own[2].wait()
+    loop(n_cent, lambda k: near_copy(k, (cent + k) % n_cent).wait_recv())
+    loop(n_samp, lambda k: far_copy(k, samp).start())
+    own[0].wait()
+    own[1].wait()
+    loop(n_cent, lambda k: near_copy(k, cent).wait_send())
+    loop(devices, lambda k: row_copy(k, me).wait_send())
+    loop(devices, lambda k: lab_copy(k, me).wait_send())
+    loop(n_samp, lambda k: far_copy(k, samp).wait_send())
+    loop(devices, lambda k: lab_copy(k, (me + k) % devices).wait_recv())
+    loop(devices, lambda k: row_copy(k, (me + k) % devices).wait_recv())
+    loop(n_samp, lambda k: far_copy(k, (samp + k) % n_samp).wait_recv())
+
+
+def return_kernel(n_samp, n_cent, out_ref, back_ref, own_sem, out_sem, in_sem):
+    devices = n_samp * n_cent
+    me = lax.axis_index("samp") * n_cent + lax.axis_index("cent")
+    own = pltpu.make_async_copy(out_ref.at[me], back_ref.at[me], own_sem)
+    own.start()
+    enter(n_samp, n_cent, me)
+
+    def copy(k, slot):
+        peer = (me + k) % devices
+        return pltpu.make_async_remote_copy(
+            out_ref.at[peer], back_ref.at[slot], out_sem.at[k], in_sem.at[slot],
+            device_id=who(n_cent, peer), device_id_type=MESH,
+        )
+
+    def loop(body):
+        def step(k, _):
+            body(k)
+            return 0
+        lax.fori_loop(1, devices, step, 0)
+
+    loop(lambda k: copy(k, me).start())
+    own.wait()
+    loop(lambda k: copy(k, me).wait_send())
+    loop(lambda k: copy(k, (me + k) % devices).wait_recv())
+
+
+def score_kernel(per_owner, near_ref, far_ref, tags_ref, cent_ref, rep_ref, weight_ref, x_ref, col_ref, dens_ref):
+    half = near_ref.shape[0]
+    slots = half + far_ref.shape[0]
+    x_ref[0:half, :] = near_ref[...]
+    x_ref[half:, :] = far_ref[...]
+    tags = tags_ref[...]
+    for start in range(0, slots, LANES):
+        chunk = jnp.broadcast_to(tags[:, start:start + LANES], (LANES, LANES))
+        col_ref[start:start + LANES, :] = jnp.transpose(chunk)
+    member = tags == (iota((per_owner, slots), 0) + 1).astype(F32)
+    member_bf = member.astype(BF)
+    sums = jnp.dot(member_bf, x_ref[...], preferred_element_type=F32)
+    scale = lax.rsqrt(jnp.sum(sums * sums, axis=1, keepdims=True) + EPSILON)
+    centroid = sums * scale
+    cent_ref[...] = centroid
+    high = centroid.astype(BF)
+    low = (centroid - high.astype(F32)).astype(BF)
+    block = 256
+    chunk = 512
+
+    def column(j, _):
+        at = pl.multiple_of(j * block, block)
+        right = x_ref[pl.ds(at, block), :]
+        tag = tags_ref[:, pl.ds(at, block)]
+
+        def inner(i, total):
+            top = pl.multiple_of(i * chunk, chunk)
+            gram = row_dot(x_ref[pl.ds(top, chunk), :], right)
+            left = col_ref[pl.ds(top, chunk), :]
+            same = jnp.concatenate([left] * (block // LANES), axis=1) == tag
+            part = jnp.where(same, jnp.exp(SHARPNESS * (gram - 1.0)), 0.0)
+            return total + jnp.sum(part, axis=0, keepdims=True)
+
+        dens_ref[:, pl.ds(at, block)] = lax.fori_loop(
+            0, slots // chunk, inner, jnp.zeros((1, block), F32)
+        )
+        return 0
+
+    lax.fori_loop(0, slots // block, column, 0)
+    towards = row_dot(high, x_ref[...]) + row_dot(low, x_ref[...])
+    similar = jnp.sum(jnp.where(member, towards, 0.0), axis=0, keepdims=True)
+    valid = tags > 0.0
+    density = jnp.where(valid, dens_ref[...], 1.0)
+    weight = jnp.where(valid, jnp.exp(1.0 - similar) / density, 0.0)
+    weight_ref[...] = weight
+    mixed = jnp.dot(
+        jnp.where(member, weight, 0.0).astype(BF), x_ref[...], preferred_element_type=F32
+    )
+    rep_ref[...] = mixed * lax.rsqrt(jnp.sum(mixed * mixed, axis=1, keepdims=True) + EPSILON)
+
+
+def pick_kernel(back_ref, meta_ref, keep_ref):
+    devices = back_ref.shape[0]
+    rows = meta_ref.shape[1]
+    meta = meta_ref[...]
+    dest_hot = (iota((devices, rows), 0) == meta[0:1, :]).astype(F32)
+    spread = lax.dot_general(
+        back_ref[:, 0, :], dest_hot, (((0,), (0,)), ((), ())),
+        preferred_element_type=F32, precision=lax.Precision.HIGHEST,
+    )
+    hit = iota((LANES, rows), 0) == meta[1:2, :]
+    keep_ref[...] = jnp.sum(jnp.where(hit, spread, 0.0), axis=0, keepdims=True)
 
 
 def all_pairs(arrived, arrived_tags, validity, block_size):
@@ -29,11 +269,9 @@
     return (similar.reshape(slot_count), density.reshape(slot_count))
 
 
-def on_device(embeddings, assignment, owner_map):
+def full_capacity(embeddings, assignment, owner_map):
     row_count, feature_width = embeddings.shape
-    n_samp = lax.axis_size("samp")
-    n_cent = lax.axis_size("cent")
-    devices = n_samp * n_cent
+    devices = lax.axis_size("samp") * lax.axis_size("cent")
     clusters = owner_map.shape[0]
     per_owner = clusters // devices
     capacity = 4 * row_count // devices
@@ -89,6 +327,107 @@
     return (centroid, representative, keep_weight)
 
 
+def on_device(embeddings, assignment, owner_map):
+    rows, width = embeddings.shape
+    n_samp = lax.axis_size("samp")
+    n_cent = lax.axis_size("cent")
+    devices = n_samp * n_cent
+    clusters = owner_map.shape[0]
+    per_owner = clusters // devices
+    capacity = 4 * rows // devices
+    near = capacity // 2
+    pool = capacity - near
+    vmem = pl.BlockSpec(memory_space=pltpu.VMEM)
+    anywhere = pl.BlockSpec(memory_space=pl.ANY)
+    shape = jax.ShapeDtypeStruct
+    dma = pltpu.SemaphoreType.DMA
+    send, pooled, labels, meta = pl.pallas_call(
+        functools.partial(pack_kernel, devices, near, pool),
+        out_shape=(
+            shape((devices, near, width), BF),
+            shape((pool, width), BF),
+            shape((devices, 1, LANES), F32),
+            shape((8, rows), jnp.int32),
+        ),
+        in_specs=[vmem] * 3,
+        out_specs=(vmem,) * 4,
+        name="pack",
+    )(embeddings, assignment.reshape(1, rows), owner_map.reshape(1, clusters))
+    arrived, pools, tags = pl.pallas_call(
+        functools.partial(exchange_kernel, n_samp, n_cent),
+        out_shape=(
+            shape((devices, near, width), BF),
+            shape((n_samp, n_cent, pool, width), BF),
+            shape((devices, 1, LANES), F32),
+        ),
+        in_specs=[anywhere] * 3,
+        out_specs=(anywhere,) * 3,
+        scratch_shapes=[
+            dma((3,)), dma((devices,)), dma((devices,)), dma((devices,)), dma((devices,)),
+            dma((n_cent,)), dma((n_cent,)), dma((n_samp,)), dma((n_samp,)),
+        ],
+        compiler_params=pltpu.CompilerParams(collective_id=0, has_side_effects=True),
+        name="exchange",
+    )(send, pooled, labels)
+    tags = tags[:, 0, :]
+
+    def fast(embeddings, assignment, owner_map, arrived, pools, tags, meta):
+        half = devices * near
+        slots = half + devices * pool
+        tag_row = jnp.concatenate(
+            [tags[:, :near].reshape(1, half), tags[:, near:capacity].reshape(1, slots - half)], axis=1
+        )
+        centroid, representative, weight = pl.pallas_call(
+            functools.partial(score_kernel, per_owner),
+            out_shape=(
+                shape((per_owner, width), F32),
+                shape((per_owner, width), F32),
+                shape((1, slots), F32),
+            ),
+            in_specs=[vmem] * 3,
+            out_specs=(vmem,) * 3,
+            scratch_shapes=[
+                pltpu.VMEM((slots, width), BF),
+                pltpu.VMEM((slots, LANES), F32),
+                pltpu.VMEM((1, slots), F32),
+            ],
+            name="score",
+        )(arrived.reshape(half, width), pools.reshape(slots - half, width), tag_row)
+        out = jnp.concatenate(
+            [
+                weight[:, :half].reshape(devices, near),
+                weight[:, half:].reshape(devices, pool),
+                jnp.zeros((devices, LANES - capacity), F32),
+            ],
+            axis=1,
+        )
+        back = pl.pallas_call(
+            functools.partial(return_kernel, n_samp, n_cent),
+            out_shape=shape((devices, 1, LANES), F32),
+            in_specs=[vmem],
+            out_specs=vmem,
+            scratch_shapes=[dma, dma((devices,)), dma((devices,))],
+            compiler_params=pltpu.CompilerParams(collective_id=1, has_side_effects=True),
+            name="give_back",
+        )(out.reshape(devices, 1, LANES))
+        keep = pl.pallas_call(
+            pick_kernel,
+            out_shape=shape((1, rows), F32),
+            in_specs=[vmem] * 2,
+            out_specs=vmem,
+            name="pick",
+        )(back, meta)
+        return centroid, representative, keep.reshape(rows)
+
+    def slow(embeddings, assignment, owner_map, arrived, pools, tags, meta):
+        return full_capacity(embeddings, assignment, owner_map)
+
+    spilled = jnp.max(tags[:, LANES - 1]) > 0.0
+    return lax.cond(
+        spilled, slow, fast, embeddings, assignment, owner_map, arrived, pools, tags, meta
+    )
+
+
 def solution(mesh):
     in_specs = (P(("samp", "cent"), None), P(("samp", "cent")), P())
     out_specs = (P(("samp", "cent"), None), P(("samp", "cent"), None), P(("samp", "cent")))

time: 189 us -> 108 us (0.57)
  Pallas kernels: 0 us -> 103 us
  waiting for transfers between devices: 99.6 us -> 0 us
  matrix products: 29.5 us -> 0 us
  local copies, waits for them, and re-layouts: 25 us -> 1.17 us
  starting transfers between devices: 17.5 us -> 0 us
  other arithmetic: 15.9 us -> 1.96 us
    pallas_call x0 -> x5, Pallas kernels: none -> 103 us  [the longest x1 62.6 us: on_device(): pl.pallas_call(functools.partial(exchange_kernel, n_samp, n_cent), out_sh...]
    all_to_all x3 -> x0, waiting for transfers between devices: 99.6 us -> none  [the longest x1 91.8 us: on_device(): lax.all_to_all(outgoing, ('samp', 'cent'), split_axis=0, concat_axis=0, t...]
    dot_general x6 -> x0, matrix products: 29.5 us -> none  [the longest x4 23.2 us: score_block(): jnp.einsum('rd,qd->rq', block_rows, arrived, preferred_element_type=jnp.f...]
    all_to_all x3 -> x0, starting transfers between devices: 17.5 us -> none  [the longest x1 7.33 us: on_device(): lax.all_to_all(labels, ('samp', 'cent'), split_axis=0, concat_axis=0, til...]
    scatter x2 -> x0, local copies, waits for them, and re-layouts: 11.8 us -> none  [the longest x1 8.05 us: on_device(): position = jnp.zeros((clusters,), jnp.int32).at[cluster_order].set(jnp.ar...]
    gather x3 -> x0, local copies, waits for them, and re-layouts: 10.8 us -> none  [the longest x1 4.27 us: on_device(): keep_weight = returned[slot_index]]
    sort x1 -> x0, other arithmetic: 5.88 us -> none  [on_device(): cluster_order = jnp.argsort(owner_map, stable=True)]
    scatter x1 -> x0, other arithmetic: 5.32 us -> none  [on_device(): jnp.zeros((slot_count, feature_width), jnp.bfloat16).at[slot_index]]
  transfers between devices with their start and end apart: 3 -> 0, of which waited for: 3 -> 0; matrix products, arithmetic and copies ran while one was open for 4% -> 0% of each run, Pallas kernels for 0% -> 0%
where the time goes in v1:
time: 108 us; the launch traced here: 107 us
  Pallas kernels  103 us (95%)
  other arithmetic  1.96 us (2%)
  between operations  1.34 us (1%)
  local copies, waits for them, and re-layouts  1.17 us (1%)
    pallas_call x1, Pallas kernels, on_device(): pl.pallas_call(functools.partial(exchange_kernel, n_samp, n_cent), out_sh...  62.6 us
    pallas_call x1, Pallas kernels, fast(): pl.pallas_call(functools.partial(score_kernel, per_owner), out_shape=(sha...  23.5 us
    pallas_call x1, Pallas kernels, fast(): pl.pallas_call(functools.partial(return_kernel, n_samp, n_cent), out_shap...  9.37 us
    pallas_call x1, Pallas kernels, on_device(): pl.pallas_call(functools.partial(pack_kernel, devices, near, pool), out_s...  5.5 us

profile of v1, /device:TPU:0, one launch (start us, length us, event | category | flops | bytes accessed | tf_op | source)
XLA Modules:
  0.0 107.2 jit_solution(3251795431347681063)
XLA Ops:
  0.6 0.0 copy-start.1
  0.6 0.0 copy-start.2
  0.7 0.0 copy-start
  0.7 5.5 %pack.1 = (bf16[32,32,1024]{2,1,0:T(8,128)(2,1)}, bf16[32,1024]{1,0:T(8,128)(2,1)}, f32[32,1,128]{2,1,0:T(1,128)}, s32[8,512]{1,0:T(8,128)S(1)}) custom-call(f32[512,1024]{1,0:T(8,128)} %emb_ref.1, s32[1,512]{1,0:T(1,128)} %bitcast.71, s32[1,2048]{1,0:T(1,128)} %bitcast.55), custom_call_target="tpu_custom_call" | custom-call | tf_op jit(solution)/shard_map/pack/pallas_call | solution.py:344
  6.2 62.6 %exchange.1 = (bf16[32,32,1024]{2,1,0:T(8,128)(2,1)}, bf16[8,4,32,1024]{3,2,1,0:T(8,128)(2,1)}, f32[32,1,128]{2,1,0:T(1,128)S(1)}) custom-call(bf16[32,32,1024]{2,1,0:T(8,128)(2,1)} %get-tuple-element.137.send_ref, bf16[32,1024]{1,0:T(8,128)(2,1)} %get-tuple-element.138.pool_ref, f32[32,1,128]{2,1,0:T(1,128)} %get-tuple-element.139.lab_ref), custom_call_target="tpu_custom_call" | custom-call | tf_op jit(solution)/shard_map/exchange/pallas_call | solution.py:356
  68.7 0.7 slice_reduce_fusion.3
  70.1 0.0 copy-done.1
  70.1 0.0 copy-done.2
  70.1 0.0 copy-done
  70.1 37.1 %conditional.1 = (f32[64,1024]{1,0:T(8,128)}, f32[64,1024]{1,0:T(8,128)}, f32[512]{0:T(512)}) conditional(s32[]{:T(128)} %convert_element_type.37, (bf16[32,32,1024]{2,1,0:T(8,128)(2,1)}, bf16[8,4,32,1024]{3,2,1,0:T(8,128)(2,1)}, f32[32,128]{1,0:T(8,128)S(1)}, s32[8,512]{1,0:T(8,128)S(1)}) %tuple.56, (s32[512]{0:T(512)S(1)}, s32[2048]{0:T(1024)S(1)}, ...), branch_computations={%region_1.0_spmd, %region_2.18_spmd} | conditional | flops 2698269696 | bytes 36988136 | solution.py:426
  70.1 0.1 fusion.25
  70.2 0.1 reshape.169
  70.3 0.1 reshape.168
  70.3 0.6 pad_maximum_fusion.tags_ref
  70.9 23.5 %score.1 = (f32[64,1024]{1,0:T(8,128)}, f32[64,1024]{1,0:T(8,128)}, f32[1,2048]{1,0:T(1,128)}) custom-call(bf16[1024,1024]{1,0:T(8,128)(2,1)} %bitcast.57, bf16[1024,1024]{1,0:T(8,128)(2,1)} %bitcast.58, f32[1,2048]{1,0:T(1,128)} %pad_maximum_fusion.tags_ref), custom_call_target="tpu_custom_call" | custom-call | tf_op jit(solution)/shard_map/cond/branch_0_fun/score/pallas_call | solution.py:380
  94.4 0.7 slice_reduce_fusion.1
  95.1 0.1 reshape.171
  95.2 0.1 reshape.170
  95.3 0.1 pad.2.clone
  95.4 0.7 maximum_maximum_fusion
  96.0 9.4 %give_back.1.back_ref = f32[32,1,128]{2,1,0:T(1,128)} custom-call(f32[32,1,128]{2,1,0:T(1,128)} %bitcast.61), custom_call_target="tpu_custom_call" | custom-call | tf_op jit(solution)/shard_map/cond/branch_0_fun/give_back/pallas_call | solution.py:404
  105.4 1.7 %pick.1 = f32[1,512]{1,0:T(1,128)} custom-call(f32[32,1,128]{2,1,0:T(1,128)} %give_back.1.back_ref, s32[8,512]{1,0:T(8,128)S(1)} %get-tuple-element.111.meta_ref), custom_call_target="tpu_custom_call" | custom-call | tf_op jit(solution)/shard_map/cond/branch_0_fun/pick/pallas_call | solution.py:413
  (1 shorter events, 0.0 us)
Async XLA Ops:
  0.6 69.4 %copy-start.1 = (f32[512,1024]{1,0:T(8,128)S(1)}, f32[512,1024]{1,0:T(8,128)}, u32[]{:S(2)}) copy-start(f32[512,1024]{1,0:T(8,128)} %emb_ref.1) | copy-start | bytes 6291460
  0.6 69.4 %copy-start.2 = (s32[512]{0:T(512)S(1)}, s32[512]{0:T(512)}, u32[]{:S(2)}) copy-start(s32[512]{0:T(512)} %param.8) | copy-start | bytes 6148
  0.7 69.4 %copy-start = (s32[2048]{0:T(1024)S(1)}, s32[2048]{0:T(1024)}, u32[]{:S(2)}) copy-start(s32[2048]{0:T(1024)} %param.9) | copy-start | bytes 24580

commit v2 on v0

--- a/solution.py
+++ b/solution.py
@@ -1,10 +1,288 @@
+import functools
+
 import jax
 import jax.numpy as jnp
 from jax import lax
+from jax.experimental import pallas as pl
+from jax.experimental.pallas import tpu as pltpu
 from jax.sharding import PartitionSpec as P
 
 EPSILON = 1e-06
 SHARPNESS = 8.0
+LANES = 128
+SPILL = 65536.0
+BF = jnp.bfloat16
+F32 = jnp.float32
+MESH = pl.DeviceIdType.MESH
+
+
+def iota(shape, axis):
+    return lax.broadcasted_iota(jnp.int32, shape, axis)
+
+
+def row_dot(a, b):
+    return lax.dot_general(a, b, (((1,), (1,)), ((), ())), preferred_element_type=F32)
+
+
+def pack_kernel(devices, n_cent, near, pool, emb_ref, assign_ref, owner_ref, send_ref, pool_ref, lab_ref, meta_ref):
+    rows = emb_ref.shape[0]
+    clusters = owner_ref.shape[1]
+    upper = (iota((rows, rows), 0) < iota((rows, rows), 1)).astype(BF)
+    owner = owner_ref[...]
+    owner_hot = (iota((devices, clusters), 0) == owner).astype(F32)
+    base = jnp.zeros((devices, 1), F32)
+    ranks = []
+    for start in range(0, clusters, rows):
+        part = owner_hot[:, start:start + rows]
+        before = jnp.dot(part.astype(BF), upper, preferred_element_type=F32) + base
+        ranks.append(jnp.sum(part * before, axis=0, keepdims=True))
+        base = base + jnp.sum(part, axis=1, keepdims=True)
+    rank = jnp.concatenate(ranks, axis=1)
+    assign = assign_ref[...]
+    pick = (iota((clusters, rows), 0) == assign).astype(BF)
+    which = iota((8, clusters), 0)
+    table = jnp.where(which == 0, owner.astype(F32), jnp.where(which == 1, rank, 0.0)).astype(BF)
+    found = jnp.dot(table, pick, preferred_element_type=F32)
+    dest = found[0:1, :].astype(jnp.int32)
+    label = found[1:2, :] + 1.0
+    dest_hot = (iota((devices, rows), 0) == dest).astype(F32)
+    before = jnp.dot(dest_hot.astype(BF), upper, preferred_element_type=F32)
+    within = jnp.sum(dest_hot * before, axis=0, keepdims=True)
+    over = (within >= near).astype(F32)
+    over_before = jnp.dot(
+        jnp.broadcast_to(over, (8, rows)).astype(BF), upper, preferred_element_type=F32
+    )[0:1, :]
+    excess = jnp.sum(over, axis=1, keepdims=True) > pool
+    within = within.astype(jnp.int32)
+    is_over = over > 0.0
+    pool_at = over_before.astype(jnp.int32)
+    cent = lax.axis_index("cent")
+    lanes = lab_ref.shape[2]
+    column = jnp.where(
+        is_over, n_cent * near + cent * pool + jnp.minimum(pool_at, pool - 1), cent * near + within
+    )
+    col_hot = (iota((lanes, rows), 0) == column).astype(BF)
+    labels = row_dot((dest_hot * label).astype(BF), col_hot)
+    lab_ref[:, 0, :] = labels + jnp.where(excess, SPILL, 0.0)
+    meta_ref[...] = jnp.where(iota((8, rows), 0) == 0, dest, column)
+    emb = emb_ref[...]
+    unit = (emb * lax.rsqrt(jnp.sum(emb * emb, axis=1, keepdims=True) + EPSILON)).astype(BF)
+    slot = jnp.where(is_over, -1, dest * near + within)
+    step = devices * near // 4
+    for start in range(0, devices * near, step):
+        hot = (iota((step, rows), 0) + start == slot).astype(BF)
+        out = jnp.dot(hot, unit, preferred_element_type=F32).astype(BF)
+        send_ref[start // near:(start + step) // near] = out.reshape(step // near, near, -1)
+    pool_hot = (iota((pool, rows), 0) == jnp.where(is_over, pool_at, -1)).astype(BF)
+    pool_ref[...] = jnp.dot(pool_hot, unit, preferred_element_type=F32).astype(BF)
+
+
+def who(n_cent, index):
+    return (index // n_cent, index % n_cent)
+
+
+def enter(n_samp, n_cent, me):
+    devices = n_samp * n_cent
+    barrier = pltpu.get_barrier_semaphore()
+
+    def greet(k, _):
+        pl.semaphore_signal(
+            barrier, inc=1, device_id=who(n_cent, (me + k) % devices), device_id_type=MESH
+        )
+        return 0
+
+    lax.fori_loop(1, devices, greet, 0)
+    pl.semaphore_wait(barrier, devices - 1)
+
+
+def dedup_kernel(
+    n_samp, n_cent, send_ref, pool_ref, lab_ref, cent_ref, rep_ref, back_ref, tags_ref,
+    near_ref, pools_ref, labs_ref, x_ref, col_ref, turn_ref, dens_ref, sums_ref, out_ref,
+    own_sem, row_out, row_in, lab_out, lab_in, near_out, near_in, far_out, far_in, back_out, back_in,
+):
+    samp = lax.axis_index("samp")
+    cent = lax.axis_index("cent")
+    me = samp * n_cent + cent
+    per_owner = cent_ref.shape[0]
+    near = near_ref.shape[2]
+    pool = pools_ref.shape[2]
+    width = x_ref.shape[1]
+    split = n_cent * near
+    block = n_cent * (near + pool)
+    slots = n_samp * block
+
+    def loop(low, high, body):
+        def step(k, _):
+            body(k)
+            return 0
+        lax.fori_loop(low, high, step, 0)
+
+    def target(shift, c):
+        return ((samp + shift) % n_samp, c)
+
+    def near_copy(c, slot):
+        return pltpu.make_async_remote_copy(
+            pool_ref, pools_ref.at[0, slot], near_out.at[c], near_in.at[slot],
+            device_id=(samp, c), device_id_type=MESH,
+        )
+
+    def row_copy(k, c, slot):
+        s, t = target(k, c)
+        return pltpu.make_async_remote_copy(
+            send_ref.at[s * n_cent + t], near_ref.at[k, slot], row_out.at[k, c], row_in.at[k, slot],
+            device_id=(s, t), device_id_type=MESH,
+        )
+
+    def lab_copy(k, c, slot):
+        s, t = target(k, c)
+        return pltpu.make_async_remote_copy(
+            lab_ref.at[s * n_cent + t], labs_ref.at[k, slot], lab_out.at[k, c], lab_in.at[k, slot],
+            device_id=(s, t), device_id_type=MESH,
+        )
+
+    def far_copy(k):
+        return pltpu.make_async_remote_copy(
+            pools_ref.at[0], pools_ref.at[k], far_out.at[k], far_in.at[k],
+            device_id=target(k, cent), device_id_type=MESH,
+        )
+
+    def back_copy(k, c, slot, at_c):
+        s = (samp + n_samp - k) % n_samp
+        return pltpu.make_async_remote_copy(
+            out_ref.at[k], back_ref.at[slot], back_out.at[k, c], back_in.at[k, at_c],
+            device_id=(s, c), device_id_type=MESH,
+        )
+
+    def others(k, body):
+        if k == 0:
+            loop(1, n_cent, lambda c: body((cent + c) % n_cent))
+        else:
+            loop(0, n_cent, lambda c: body((cent + c) % n_cent))
+
+    own = [
+        pltpu.make_async_copy(send_ref.at[me], near_ref.at[0, cent], own_sem.at[0]),
+        pltpu.make_async_copy(lab_ref.at[me], labs_ref.at[0, cent], own_sem.at[1]),
+        pltpu.make_async_copy(pool_ref, pools_ref.at[0, cent], own_sem.at[2]),
+    ]
+    for copy in own:
+        copy.start()
+    enter(n_samp, n_cent, me)
+
+    def rows_start(k):
+        others(k, lambda c: lab_copy(k, c, cent).start())
+        others(k, lambda c: row_copy(k, c, cent).start())
+
+    others(0, lambda c: near_copy(c, cent).start())
+    rows_start(0)
+    rows_start(1)
+    turn_ref[...] = jnp.zeros_like(turn_ref)
+    own[2].wait()
+    others(0, lambda c: near_copy(c, c).wait_recv())
+    far_copy(1).start()
+    for k in range(2, n_samp):
+        rows_start(k)
+        far_copy(k).start()
+    own[0].wait()
+    own[1].wait()
+    sums_ref[...] = jnp.zeros_like(sums_ref)
+    for k in range(n_samp):
+        at = k * block
+        others(k, lambda c: lab_copy(k, c, c).wait_recv())
+        others(k, lambda c: row_copy(k, c, c).wait_recv())
+        if k > 0:
+            far_copy(k).wait_recv()
+        x_ref[at:at + split, :] = near_ref[k].reshape(split, width)
+        x_ref[at + split:at + block, :] = pools_ref[k].reshape(block - split, width)
+        tag = jnp.sum(labs_ref[k], axis=0)
+        tags_ref[k] = tag
+        for start in range(0, block, LANES):
+            chunk = jnp.broadcast_to(tag[:, start:start + LANES], (LANES, LANES))
+            col_ref[at + start:at + start + LANES, :] = jnp.transpose(chunk)
+        fresh = x_ref[at:at + block, :]
+        member = (tag == (iota((per_owner, block), 0) + 1).astype(F32)).astype(BF)
+        sums_ref[...] += jnp.dot(member, fresh, preferred_element_type=F32)
+
+        def piece(top, height):
+            gram = row_dot(x_ref[pl.ds(top, height), :], fresh)
+            left = col_ref[pl.ds(top, height), :]
+            same = jnp.concatenate([left] * (block // LANES), axis=1) == tag
+            return jnp.where(same, jnp.exp(SHARPNESS * (gram - 1.0)), 0.0)
+
+        def both(top, height):
+            part = piece(top, height)
+            folded = part[:, 0:LANES]
+            for start in range(LANES, block, LANES):
+                folded = folded + part[:, start:start + LANES]
+            turn_ref[pl.ds(top, height), :] += folded
+            return jnp.sum(part, axis=0, keepdims=True)
+
+        total = jnp.sum(piece(at, block), axis=0, keepdims=True)
+        if k >= 2:
+            total = lax.fori_loop(
+                0, k // 2,
+                lambda j, t: t + both(pl.multiple_of(j * 2 * block, 2 * block), 2 * block),
+                total,
+            )
+        if k % 2:
+            total = total + both((k - 1) * block, block)
+        dens_ref[k] = total
+    sums = sums_ref[...]
+    scale = lax.rsqrt(jnp.sum(sums * sums, axis=1, keepdims=True) + EPSILON)
+    centroid = sums * scale
+    cent_ref[...] = centroid
+    high = centroid.astype(BF)
+    low = (centroid - high.astype(F32)).astype(BF)
+    pair = jnp.concatenate([high, low], axis=0)
+    for k in range(n_samp):
+        at = k * block
+        tag = tags_ref[k]
+        valid = tag > 0.0
+        member = tag == (iota((per_owner, block), 0) + 1).astype(F32)
+        towards = row_dot(pair, x_ref[at:at + block, :])
+        towards = towards[0:per_owner, :] + towards[per_owner:, :]
+        similar = jnp.sum(jnp.where(member, towards, 0.0), axis=0, keepdims=True)
+        flipped = []
+        for start in range(at, at + block, LANES):
+            flipped.append(
+                jnp.sum(jnp.transpose(turn_ref[start:start + LANES, :]), axis=0, keepdims=True)
+            )
+        density = jnp.where(valid, dens_ref[k] + jnp.concatenate(flipped, axis=1), 1.0)
+        out_ref[k] = jnp.where(valid, jnp.exp(1.0 - similar) / density, 0.0)
+    mine = pltpu.make_async_copy(out_ref.at[0], back_ref.at[me], own_sem.at[3])
+    mine.start()
+    mine.wait()
+    for k in range(n_samp):
+        others(k, lambda c: back_copy(k, c, me, cent).start())
+    mixed = jnp.zeros(sums_ref.shape, F32)
+    for k in range(n_samp):
+        member = tags_ref[k] == (iota((per_owner, block), 0) + 1).astype(F32)
+        mixed = mixed + jnp.dot(
+            jnp.where(member, out_ref[k], 0.0).astype(BF), x_ref[k * block:(k + 1) * block, :],
+            preferred_element_type=F32,
+        )
+    rep_ref[...] = mixed * lax.rsqrt(jnp.sum(mixed * mixed, axis=1, keepdims=True) + EPSILON)
+    others(0, lambda c: near_copy(c, cent).wait_send())
+    for k in range(n_samp):
+        others(k, lambda c: lab_copy(k, c, cent).wait_send())
+        others(k, lambda c: row_copy(k, c, cent).wait_send())
+        if k > 0:
+            far_copy(k).wait_send()
+        others(k, lambda c: back_copy(k, c, me, cent).wait_send())
+    for k in range(n_samp):
+        others(k, lambda c: back_copy(k, c, ((samp + k) % n_samp) * n_cent + c, c).wait_recv())
+
+
+def pick_kernel(back_ref, meta_ref, keep_ref):
+    devices = back_ref.shape[0]
+    rows = meta_ref.shape[1]
+    meta = meta_ref[...]
+    dest_hot = (iota((devices, rows), 0) == meta[0:1, :]).astype(F32)
+    spread = lax.dot_general(
+        back_ref[:, 0, :], dest_hot, (((0,), (0,)), ((), ())),
+        preferred_element_type=F32, precision=lax.Precision.HIGHEST,
+    )
+    hit = iota((back_ref.shape[2], rows), 0) == meta[1:2, :]
+    keep_ref[...] = jnp.sum(jnp.where(hit, spread, 0.0), axis=0, keepdims=True)
 
 
 def all_pairs(arrived, arrived_tags, validity, block_size):
@@ -29,11 +307,9 @@
     return (similar.reshape(slot_count), density.reshape(slot_count))
 
 
-def on_device(embeddings, assignment, owner_map):
+def full_capacity(embeddings, assignment, owner_map):
     row_count, feature_width = embeddings.shape
-    n_samp = lax.axis_size("samp")
-    n_cent = lax.axis_size("cent")
-    devices = n_samp * n_cent
+    devices = lax.axis_size("samp") * lax.axis_size("cent")
     clusters = owner_map.shape[0]
     per_owner = clusters // devices
     capacity = 4 * row_count // devices
@@ -89,6 +365,82 @@
     return (centroid, representative, keep_weight)
 
 
+def on_device(embeddings, assignment, owner_map):
+    rows, width = embeddings.shape
+    n_samp = lax.axis_size("samp")
+    n_cent = lax.axis_size("cent")
+    devices = n_samp * n_cent
+    clusters = owner_map.shape[0]
+    per_owner = clusters // devices
+    capacity = 4 * rows // devices
+    near = capacity // 2
+    pool = capacity - near
+    vmem = pl.BlockSpec(memory_space=pltpu.VMEM)
+    anywhere = pl.BlockSpec(memory_space=pl.ANY)
+    shape = jax.ShapeDtypeStruct
+    dma = pltpu.SemaphoreType.DMA
+    block = n_cent * capacity
+    slots = n_samp * block
+    send, pooled, labels, meta = pl.pallas_call(
+        functools.partial(pack_kernel, devices, n_cent, near, pool),
+        out_shape=(
+            shape((devices, near, width), BF),
+            shape((pool, width), BF),
+            shape((devices, 1, block), F32),
+            shape((8, rows), jnp.int32),
+        ),
+        in_specs=[vmem] * 3,
+        out_specs=(vmem,) * 4,
+        name="pack",
+    )(embeddings, assignment.reshape(1, rows), owner_map.reshape(1, clusters))
+    centroid, representative, back, tags = pl.pallas_call(
+        functools.partial(dedup_kernel, n_samp, n_cent),
+        out_shape=(
+            shape((per_owner, width), F32),
+            shape((per_owner, width), F32),
+            shape((devices, 1, block), F32),
+            shape((n_samp, 1, block), F32),
+        ),
+        in_specs=[anywhere] * 3,
+        out_specs=(vmem,) * 4,
+        scratch_shapes=[
+            pltpu.VMEM((n_samp, n_cent, near, width), BF),
+            pltpu.VMEM((n_samp, n_cent, pool, width), BF),
+            pltpu.VMEM((n_samp, n_cent, 1, block), F32),
+            pltpu.VMEM((slots, width), BF),
+            pltpu.VMEM((slots, LANES), F32),
+            pltpu.VMEM((slots, LANES), F32),
+            pltpu.VMEM((n_samp, 1, block), F32),
+            pltpu.VMEM((per_owner, width), F32),
+            pltpu.VMEM((n_samp, 1, block), F32),
+            dma((4,)),
+            dma((n_samp, n_cent)), dma((n_samp, n_cent)), dma((n_samp, n_cent)), dma((n_samp, n_cent)),
+            dma((n_cent,)), dma((n_cent,)), dma((n_samp,)), dma((n_samp,)),
+            dma((n_samp, n_cent)), dma((n_samp, n_cent)),
+        ],
+        compiler_params=pltpu.CompilerParams(collective_id=0, has_side_effects=True),
+        name="dedup",
+    )(send, pooled, labels)
+    keep = pl.pallas_call(
+        pick_kernel,
+        out_shape=shape((1, rows), F32),
+        in_specs=[vmem] * 2,
+        out_specs=vmem,
+        name="pick",
+    )(back, meta).reshape(rows)
+
+    def fast(embeddings, assignment, owner_map, centroid, representative, keep):
+        return centroid, representative, keep
+
+    def slow(embeddings, assignment, owner_map, centroid, representative, keep):
+        return full_capacity(embeddings, assignment, owner_map)
+
+    spilled = jnp.max(tags) >= SPILL
+    return lax.cond(
+        spilled, slow, fast, embeddings, assignment, owner_map, centroid, representative, keep
+    )
+
+
 def solution(mesh):
     in_specs = (P(("samp", "cent"), None), P(("samp", "cent")), P())
     out_specs = (P(("samp", "cent"), None), P(("samp", "cent"), None), P(("samp", "cent")))

time: 189 us -> 89.5 us (0.47)
  waiting for transfers between devices: 99.6 us -> 0 us
  Pallas kernels: 0 us -> 85 us
  matrix products: 29.5 us -> 0 us
  local copies, waits for them, and re-layouts: 25 us -> 1.43 us
  starting transfers between devices: 17.5 us -> 0 us
  other arithmetic: 15.9 us -> 1.32 us
    all_to_all x3 -> x0, waiting for transfers between devices: 99.6 us -> none  [the longest x1 91.8 us: on_device(): lax.all_to_all(outgoing, ('samp', 'cent'), split_axis=0, concat_axis=0, t...]
    pallas_call x0 -> x3, Pallas kernels: none -> 85 us  [the longest x1 78 us: on_device(): pl.pallas_call(functools.partial(dedup_kernel, n_samp, n_cent), out_shape...]
    dot_general x6 -> x0, matrix products: 29.5 us -> none  [the longest x4 23.2 us: score_block(): jnp.einsum('rd,qd->rq', block_rows, arrived, preferred_element_type=jnp.f...]
    all_to_all x3 -> x0, starting transfers between devices: 17.5 us -> none  [the longest x1 7.33 us: on_device(): lax.all_to_all(labels, ('samp', 'cent'), split_axis=0, concat_axis=0, til...]
    scatter x2 -> x0, local copies, waits for them, and re-layouts: 11.8 us -> none  [the longest x1 8.05 us: on_device(): position = jnp.zeros((clusters,), jnp.int32).at[cluster_order].set(jnp.ar...]
    gather x3 -> x0, local copies, waits for them, and re-layouts: 10.8 us -> none  [the longest x1 4.27 us: on_device(): keep_weight = returned[slot_index]]
    sort x1 -> x0, other arithmetic: 5.88 us -> none  [on_device(): cluster_order = jnp.argsort(owner_map, stable=True)]
    scatter x1 -> x0, other arithmetic: 5.32 us -> none  [on_device(): jnp.zeros((slot_count, feature_width), jnp.bfloat16).at[slot_index]]
  transfers between devices with their start and end apart: 3 -> 0, of which waited for: 3 -> 0; matrix products, arithmetic and copies ran while one was open for 4% -> 0% of each run, Pallas kernels for 0% -> 0%
where the time goes in v2:
time: 89.5 us; the launch traced here: 89.3 us
  Pallas kernels  85 us (95%)
  local copies, waits for them, and re-layouts  1.43 us (2%)
  between operations  1.36 us (2%)
  other arithmetic  1.32 us (1%)
    pallas_call x1, Pallas kernels, on_device(): pl.pallas_call(functools.partial(dedup_kernel, n_samp, n_cent), out_shape...  78 us
    pallas_call x1, Pallas kernels, on_device(): pl.pallas_call(functools.partial(pack_kernel, devices, n_cent, near, pool...  5.59 us

profile of v2, /device:TPU:0, one launch (start us, length us, event | category | flops | bytes accessed | tf_op | source)
XLA Modules:
  0.0 89.3 jit_solution(635466281987490737)
XLA Ops:
  0.6 0.0 copy-start.1
  0.6 0.0 copy-start.2
  0.7 0.0 copy-start
  0.7 5.6 %pack.1 = (bf16[32,32,1024]{2,1,0:T(8,128)(2,1)}, bf16[32,1024]{1,0:T(8,128)(2,1)}, f32[32,1,256]{2,1,0:T(1,128)}, s32[8,512]{1,0:T(8,128)}) custom-call(f32[512,1024]{1,0:T(8,128)} %emb_ref.1, s32[1,512]{1,0:T(1,128)} %bitcast.62, s32[1,2048]{1,0:T(1,128)} %bitcast.51), custom_call_target="tpu_custom_call" | custom-call | tf_op jit(solution)/shard_map/pack/pallas_call | solution.py:384
  6.2 78.0 %dedup.1 = (f32[64,1024]{1,0:T(8,128)S(1)}, f32[64,1024]{1,0:T(8,128)S(1)}, f32[32,1,256]{2,1,0:T(1,128)}, f32[8,1,256]{2,1,0:T(1,128)}) custom-call(bf16[32,32,1024]{2,1,0:T(8,128)(2,1)} %get-tuple-element.136.send_ref, bf16[32,1024]{1,0:T(8,128)(2,1)} %get-tuple-element.137.pool_ref, f32[32,1,256]{2,1,0:T(1,128)} %get-tuple-element.138.lab_ref), custom_call_target="tpu_custom_call" | custom-call | tf_op jit(solution)/shard_map/dedup/pallas_call | solution.py:396
  84.2 1.3 %reduce_max.9 = f32[]{:T(128)} reduce(f32[8,1,256]{2,1,0:T(1,128)} %get-tuple-element.139, f32[]{:T(128)} %constant.72.clone.1), dimensions={0,1,2}, to_apply=%region_0.0 | reduce | flops 2047 | bytes 8200 | tf_op jit(solution)/shard_map/reduce_max | solution.py:438
  86.2 1.4 %pick.1 = f32[1,512]{1,0:T(1,128)S(1)} custom-call(f32[32,1,256]{2,1,0:T(1,128)} %get-tuple-element.140.back_ref, s32[8,512]{1,0:T(8,128)} %get-tuple-element.141.meta_ref), custom_call_target="tpu_custom_call" | custom-call | tf_op jit(solution)/shard_map/pick/pallas_call | solution.py:424
  87.6 0.0 copy-done.1
  87.6 0.0 copy-done.2
  87.6 0.0 copy-done
  87.6 0.2 conditional.1
  87.9 0.0 copy-start.3
  87.9 0.7 copy.38
  88.6 0.7 copy.39
  89.3 0.0 copy-done.3
Async XLA Ops:
  0.6 87.0 %copy-start.1 = (f32[512,1024]{1,0:T(8,128)S(1)}, f32[512,1024]{1,0:T(8,128)}, u32[]{:S(2)}) copy-start(f32[512,1024]{1,0:T(8,128)} %emb_ref.1) | copy-start | bytes 6291460
  0.6 87.0 %copy-start.2 = (s32[512]{0:T(512)S(1)}, s32[512]{0:T(512)}, u32[]{:S(2)}) copy-start(s32[512]{0:T(512)} %param.8) | copy-start | bytes 6148
  0.7 87.0 %copy-start = (s32[2048]{0:T(1024)S(1)}, s32[2048]{0:T(1024)}, u32[]{:S(2)}) copy-start(s32[2048]{0:T(1024)} %param.9) | copy-start | bytes 24580
  87.9 1.4 %copy-start.3 = (f32[512]{0:T(512)}, f32[512]{0:T(512)S(1)}, u32[]{:S(2)}) copy-start(f32[512]{0:T(512)S(1)} %get-tuple-element.270) | copy-start | bytes 6148

commit v3 on v2

--- a/solution.py
+++ b/solution.py
@@ -24,7 +24,11 @@
     return lax.dot_general(a, b, (((1,), (1,)), ((), ())), preferred_element_type=F32)
 
 
-def pack_kernel(devices, n_cent, near, pool, emb_ref, assign_ref, owner_ref, send_ref, pool_ref, lab_ref, meta_ref):
+def samp_half(shift):
+    return (shift // 2) % 2
+
+
+def pack_kernel(devices, n_cent, near, pool, emb_ref, assign_ref, owner_ref, send_ref, pool_ref, index_ref, lab_ref, meta_ref):
     rows = emb_ref.shape[0]
     clusters = owner_ref.shape[1]
     upper = (iota((rows, rows), 0) < iota((rows, rows), 1)).astype(BF)
@@ -56,23 +60,34 @@
     within = within.astype(jnp.int32)
     is_over = over > 0.0
     pool_at = over_before.astype(jnp.int32)
+    samp = lax.axis_index("samp")
     cent = lax.axis_index("cent")
-    lanes = lab_ref.shape[2]
-    column = jnp.where(
-        is_over, n_cent * near + cent * pool + jnp.minimum(pool_at, pool - 1), cent * near + within
-    )
-    col_hot = (iota((lanes, rows), 0) == column).astype(BF)
+    n_samp = devices // n_cent
+    span = n_samp * near
+    shift = (dest // n_cent + n_samp - samp) % n_samp
+    toward = dest % n_cent
+    near_lane = shift * near + within
+    pair_lane = (samp_half(shift) * n_cent + cent) * pool + jnp.minimum(pool_at, pool - 1)
+    column = jnp.where(is_over, span + pair_lane, near_lane)
+    col_hot = (iota((lab_ref.shape[2], rows), 0) == column).astype(BF)
     labels = row_dot((dest_hot * label).astype(BF), col_hot)
-    lab_ref[:, 0, :] = labels + jnp.where(excess, SPILL, 0.0)
+    lane_hot = (iota((n_cent, rows), 0) == jnp.where(is_over, -1, toward)).astype(F32)
+    lane_before = jnp.dot(lane_hot.astype(BF), upper, preferred_element_type=F32)
+    packed = jnp.sum(lane_hot * lane_before, axis=0, keepdims=True).astype(jnp.int32)
+    limit = send_ref.shape[1]
+    crowded = jnp.sum(
+        jnp.where((packed >= limit) & jnp.logical_not(is_over), 1.0, 0.0), axis=1, keepdims=True
+    ) > 0.0
+    lab_ref[:, 0, :] = labels + jnp.where(excess | crowded, SPILL, 0.0)
+    seat_hot = (iota((index_ref.shape[2], rows), 0) == packed).astype(BF)
+    index_ref[:, 0, :] = row_dot((lane_hot * (near_lane + 1).astype(F32)).astype(BF), seat_hot)
     meta_ref[...] = jnp.where(iota((8, rows), 0) == 0, dest, column)
     emb = emb_ref[...]
     unit = (emb * lax.rsqrt(jnp.sum(emb * emb, axis=1, keepdims=True) + EPSILON)).astype(BF)
-    slot = jnp.where(is_over, -1, dest * near + within)
-    step = devices * near // 4
-    for start in range(0, devices * near, step):
-        hot = (iota((step, rows), 0) + start == slot).astype(BF)
-        out = jnp.dot(hot, unit, preferred_element_type=F32).astype(BF)
-        send_ref[start // near:(start + step) // near] = out.reshape(step // near, near, -1)
+    seat = jnp.where(is_over, -1, jnp.where(packed < limit, toward * limit + packed, -1))
+    for c in range(n_cent):
+        hot = (iota((limit, rows), 0) + c * limit == seat).astype(BF)
+        send_ref[c] = jnp.dot(hot, unit, preferred_element_type=F32).astype(BF)
     pool_hot = (iota((pool, rows), 0) == jnp.where(is_over, pool_at, -1)).astype(BF)
     pool_ref[...] = jnp.dot(pool_hot, unit, preferred_element_type=F32).astype(BF)
 
@@ -96,9 +111,11 @@
 
 
 def dedup_kernel(
-    n_samp, n_cent, send_ref, pool_ref, lab_ref, cent_ref, rep_ref, back_ref, tags_ref,
-    near_ref, pools_ref, labs_ref, x_ref, col_ref, turn_ref, dens_ref, sums_ref, out_ref,
+    n_samp, n_cent, send_ref, pool_ref, index_ref, lab_ref, cent_ref, rep_ref, back_ref, tags_ref,
+    lane_ref, seat_ref, stage_ref, near_ref, pools_ref, labs_ref, x_ref, col_ref, turn_ref, dens_ref,
+    sums_ref, out_ref,
     own_sem, row_out, row_in, lab_out, lab_in, near_out, near_in, far_out, far_in, back_out, back_in,
+    lane_out, lane_in, seat_out, seat_in, fwd_out,
 ):
     samp = lax.axis_index("samp")
     cent = lax.axis_index("cent")
@@ -107,9 +124,12 @@
     near = near_ref.shape[2]
     pool = pools_ref.shape[2]
     width = x_ref.shape[1]
-    split = n_cent * near
-    block = n_cent * (near + pool)
-    slots = n_samp * block
+    limit = lane_ref.shape[1]
+    span = n_samp * near
+    block = span
+    quads = n_samp // 2
+    count = n_cent + quads
+    evens = list(range(0, n_samp, 2))
 
     def loop(low, high, body):
         def step(k, _):
@@ -126,11 +146,22 @@
             device_id=(samp, c), device_id_type=MESH,
         )
 
-    def row_copy(k, c, slot):
-        s, t = target(k, c)
-        return pltpu.make_async_remote_copy(
-            send_ref.at[s * n_cent + t], near_ref.at[k, slot], row_out.at[k, c], row_in.at[k, slot],
-            device_id=(s, t), device_id_type=MESH,
+    def lane_copy(c, slot):
+        return pltpu.make_async_remote_copy(
+            send_ref.at[c], lane_ref.at[slot], lane_out.at[c], lane_in.at[slot],
+            device_id=(samp, c), device_id_type=MESH,
+        )
+
+    def seat_copy(c, slot):
+        return pltpu.make_async_remote_copy(
+            index_ref.at[c], seat_ref.at[slot], seat_out.at[c], seat_in.at[slot],
+            device_id=(samp, c), device_id_type=MESH,
+        )
+
+    def row_copy(k, c):
+        return pltpu.make_async_remote_copy(
+            stage_ref.at[c, k], near_ref.at[c, k], row_out.at[k, c], row_in.at[k, c],
+            device_id=target(k, cent), device_id_type=MESH,
         )
 
     def lab_copy(k, c, slot):
@@ -146,55 +177,69 @@
             device_id=target(k, cent), device_id_type=MESH,
         )
 
+    turn_by = 1 + (n_samp - 2) * (samp % 2)
+
+    def forward(k):
+        slot = (k + turn_by) % n_samp
+        return pltpu.make_async_remote_copy(
+            pools_ref.at[k], pools_ref.at[slot], fwd_out.at[k], far_in.at[slot],
+            device_id=target(turn_by, cent), device_id_type=MESH,
+        )
+
     def back_copy(k, c, slot, at_c):
         s = (samp + n_samp - k) % n_samp
         return pltpu.make_async_remote_copy(
-            out_ref.at[k], back_ref.at[slot], back_out.at[k, c], back_in.at[k, at_c],
+            out_ref.at[c, samp_pair(k)], back_ref.at[slot], back_out.at[k, c], back_in.at[k, at_c],
             device_id=(s, c), device_id_type=MESH,
         )
 
+    def samp_pair(k):
+        return (k // 4) + (k % 2) * (n_samp // 4)
+
     def others(k, body):
-        if k == 0:
-            loop(1, n_cent, lambda c: body((cent + c) % n_cent))
-        else:
-            loop(0, n_cent, lambda c: body((cent + c) % n_cent))
+        loop(1 if k == 0 else 0, n_cent, lambda c: body((cent + c) % n_cent))
 
     own = [
-        pltpu.make_async_copy(send_ref.at[me], near_ref.at[0, cent], own_sem.at[0]),
+        pltpu.make_async_copy(send_ref.at[cent], lane_ref.at[cent], own_sem.at[0]),
         pltpu.make_async_copy(lab_ref.at[me], labs_ref.at[0, cent], own_sem.at[1]),
         pltpu.make_async_copy(pool_ref, pools_ref.at[0, cent], own_sem.at[2]),
+        pltpu.make_async_copy(index_ref.at[cent], seat_ref.at[cent], own_sem.at[3]),
     ]
     for copy in own:
         copy.start()
     enter(n_samp, n_cent, me)
-
-    def rows_start(k):
+    others(0, lambda c: seat_copy(c, cent).start())
+    others(0, lambda c: near_copy(c, cent).start())
+    others(0, lambda c: lane_copy(c, cent).start())
+    for k in range(n_samp):
         others(k, lambda c: lab_copy(k, c, cent).start())
-        others(k, lambda c: row_copy(k, c, cent).start())
-
-    others(0, lambda c: near_copy(c, cent).start())
-    rows_start(0)
-    rows_start(1)
     turn_ref[...] = jnp.zeros_like(turn_ref)
-    own[2].wait()
+    sums_ref[...] = jnp.zeros_like(sums_ref)
+    for copy in own:
+        copy.wait()
+
+    def spread(c):
+        seat = seat_ref[c][:, 0:limit].astype(jnp.int32)
+        hot = (iota((span, limit), 0) + 1 == seat).astype(BF)
+        rows = jnp.dot(hot, lane_ref[c], preferred_element_type=F32).astype(BF)
+        stage_ref[c] = rows.reshape(n_samp, near, width)
+
+    def pass_on(c):
+        loop(1, n_samp, lambda k: row_copy(k, c).start())
+
+    spread(cent)
     others(0, lambda c: near_copy(c, c).wait_recv())
-    far_copy(1).start()
-    for k in range(2, n_samp):
-        rows_start(k)
+    pass_on(cent)
+    for k in evens[1:]:
         far_copy(k).start()
-    own[0].wait()
-    own[1].wait()
-    sums_ref[...] = jnp.zeros_like(sums_ref)
+    forward(0).start()
     for k in range(n_samp):
-        at = k * block
         others(k, lambda c: lab_copy(k, c, c).wait_recv())
-        others(k, lambda c: row_copy(k, c, c).wait_recv())
-        if k > 0:
-            far_copy(k).wait_recv()
-        x_ref[at:at + split, :] = near_ref[k].reshape(split, width)
-        x_ref[at + split:at + block, :] = pools_ref[k].reshape(block - split, width)
-        tag = jnp.sum(labs_ref[k], axis=0)
-        tags_ref[k] = tag
+
+    def score(p, load, tag):
+        at = p * block
+        load(at)
+        tags_ref[p] = tag
         for start in range(0, block, LANES):
             chunk = jnp.broadcast_to(tag[:, start:start + LANES], (LANES, LANES))
             col_ref[at + start:at + start + LANES, :] = jnp.transpose(chunk)
@@ -217,15 +262,62 @@
             return jnp.sum(part, axis=0, keepdims=True)
 
         total = jnp.sum(piece(at, block), axis=0, keepdims=True)
-        if k >= 2:
+        if p >= 2:
             total = lax.fori_loop(
-                0, k // 2,
+                0, p // 2,
                 lambda j, t: t + both(pl.multiple_of(j * 2 * block, 2 * block), 2 * block),
                 total,
             )
-        if k % 2:
-            total = total + both((k - 1) * block, block)
-        dens_ref[k] = total
+        if p % 2:
+            total = total + both((p - 1) * block, block)
+        dens_ref[p] = total
+
+    def near_block(p, i):
+        c = (cent + i) % n_cent
+        tag = labs_ref[0, c][:, 0:span]
+        for k in range(1, n_samp):
+            tag = tag + labs_ref[k, c][:, 0:span]
+        loop(1, n_samp, lambda k: row_copy(k, c).wait_recv())
+
+        def load(at):
+            x_ref[at:at + near, :] = stage_ref[c, 0]
+            x_ref[at + near:at + block, :] = near_ref[c, 1:].reshape(block - near, width)
+
+        score(p, load, tag)
+
+    def pool_block(p, q):
+        first = 4 * (q % (n_samp // 4)) + q // (n_samp // 4)
+        half = n_cent * pool
+        tag = jnp.zeros((1, block), F32)
+        for k in (first, first + 2):
+            for c in range(n_cent):
+                tag = tag + labs_ref[k, c][:, span:span + block]
+            if k > 0:
+                far_copy(k).wait_recv()
+                if k % 2 == 0:
+                    forward(k).start()
+
+        def load(at):
+            x_ref[at:at + half, :] = pools_ref[first].reshape(half, width)
+            x_ref[at + half:at + block, :] = pools_ref[first + 2].reshape(half, width)
+
+        score(p, load, tag)
+
+    for i in range(1, n_cent):
+        c = (cent + i) % n_cent
+        seat_copy(c, c).wait_recv()
+        lane_copy(c, c).wait_recv()
+        spread(c)
+        pass_on(c)
+    order = [(True, 0)] + [(False, q) for q in range(quads // 2)]
+    order += [(True, i) for i in range(1, n_cent)]
+    order += [(False, q) for q in range(quads // 2, quads)]
+    for p, (is_near, which) in enumerate(order):
+        if is_near:
+            near_block(p, which)
+        else:
+            pool_block(p, which)
+
     sums = sums_ref[...]
     scale = lax.rsqrt(jnp.sum(sums * sums, axis=1, keepdims=True) + EPSILON)
     centroid = sums * scale
@@ -233,9 +325,9 @@
     high = centroid.astype(BF)
     low = (centroid - high.astype(F32)).astype(BF)
     pair = jnp.concatenate([high, low], axis=0)
-    for k in range(n_samp):
-        at = k * block
-        tag = tags_ref[k]
+    for p in range(count):
+        at = p * block
+        tag = tags_ref[p]
         valid = tag > 0.0
         member = tag == (iota((per_owner, block), 0) + 1).astype(F32)
         towards = row_dot(pair, x_ref[at:at + block, :])
@@ -246,27 +338,40 @@
             flipped.append(
                 jnp.sum(jnp.transpose(turn_ref[start:start + LANES, :]), axis=0, keepdims=True)
             )
-        density = jnp.where(valid, dens_ref[k] + jnp.concatenate(flipped, axis=1), 1.0)
-        out_ref[k] = jnp.where(valid, jnp.exp(1.0 - similar) / density, 0.0)
-    mine = pltpu.make_async_copy(out_ref.at[0], back_ref.at[me], own_sem.at[3])
+        density = jnp.where(valid, dens_ref[p] + jnp.concatenate(flipped, axis=1), 1.0)
+        weight = jnp.where(valid, jnp.exp(1.0 - similar) / density, 0.0)
+        dens_ref[p] = weight
+        is_near, which = order[p]
+        if is_near:
+            c = (cent + which) % n_cent
+            for q in range(quads):
+                out_ref[c, q, :, 0:span] = weight
+        else:
+            for c in range(n_cent):
+                out_ref[c, which, :, span:span + block] = weight
+    mine = pltpu.make_async_copy(out_ref.at[cent, 0], back_ref.at[me], own_sem.at[4])
     mine.start()
     mine.wait()
     for k in range(n_samp):
         others(k, lambda c: back_copy(k, c, me, cent).start())
     mixed = jnp.zeros(sums_ref.shape, F32)
-    for k in range(n_samp):
-        member = tags_ref[k] == (iota((per_owner, block), 0) + 1).astype(F32)
+    for p in range(count):
+        member = tags_ref[p] == (iota((per_owner, block), 0) + 1).astype(F32)
         mixed = mixed + jnp.dot(
-            jnp.where(member, out_ref[k], 0.0).astype(BF), x_ref[k * block:(k + 1) * block, :],
+            jnp.where(member, dens_ref[p], 0.0).astype(BF), x_ref[p * block:(p + 1) * block, :],
             preferred_element_type=F32,
         )
     rep_ref[...] = mixed * lax.rsqrt(jnp.sum(mixed * mixed, axis=1, keepdims=True) + EPSILON)
+    others(0, lambda c: seat_copy(c, cent).wait_send())
     others(0, lambda c: near_copy(c, cent).wait_send())
+    others(0, lambda c: lane_copy(c, cent).wait_send())
+    loop(0, n_cent, lambda c: loop(1, n_samp, lambda k: row_copy(k, c).wait_send()))
     for k in range(n_samp):
         others(k, lambda c: lab_copy(k, c, cent).wait_send())
-        others(k, lambda c: row_copy(k, c, cent).wait_send())
-        if k > 0:
-            far_copy(k).wait_send()
+        if k % 2 == 0:
+            forward(k).wait_send()
+            if k > 0:
+                far_copy(k).wait_send()
         others(k, lambda c: back_copy(k, c, me, cent).wait_send())
     for k in range(n_samp):
         others(k, lambda c: back_copy(k, c, ((samp + k) % n_samp) * n_cent + c, c).wait_recv())
@@ -379,18 +484,22 @@
     anywhere = pl.BlockSpec(memory_space=pl.ANY)
     shape = jax.ShapeDtypeStruct
     dma = pltpu.SemaphoreType.DMA
-    block = n_cent * capacity
-    slots = n_samp * block
-    send, pooled, labels, meta = pl.pallas_call(
+    block = n_samp * near
+    blocks = n_cent + n_samp // 2
+    slots = blocks * block
+    limit = 21 * block // 32 // 8 * 8
+    room = (limit + LANES - 1) // LANES * LANES
+    send, pooled, index, labels, meta = pl.pallas_call(
         functools.partial(pack_kernel, devices, n_cent, near, pool),
         out_shape=(
-            shape((devices, near, width), BF),
+            shape((n_cent, limit, width), BF),
             shape((pool, width), BF),
-            shape((devices, 1, block), F32),
+            shape((n_cent, 1, room), F32),
+            shape((devices, 1, 2 * block), F32),
             shape((8, rows), jnp.int32),
         ),
         in_specs=[vmem] * 3,
-        out_specs=(vmem,) * 4,
+        out_specs=(vmem,) * 5,
         name="pack",
     )(embeddings, assignment.reshape(1, rows), owner_map.reshape(1, clusters))
     centroid, representative, back, tags = pl.pallas_call(
@@ -398,29 +507,33 @@
         out_shape=(
             shape((per_owner, width), F32),
             shape((per_owner, width), F32),
-            shape((devices, 1, block), F32),
-            shape((n_samp, 1, block), F32),
+            shape((devices, 1, 2 * block), F32),
+            shape((blocks, 1, block), F32),
         ),
-        in_specs=[anywhere] * 3,
+        in_specs=[anywhere] * 4,
         out_specs=(vmem,) * 4,
         scratch_shapes=[
-            pltpu.VMEM((n_samp, n_cent, near, width), BF),
+            pltpu.VMEM((n_cent, limit, width), BF),
+            pltpu.VMEM((n_cent, 1, room), F32),
+            pltpu.VMEM((n_cent, n_samp, near, width), BF),
+            pltpu.VMEM((n_cent, n_samp, near, width), BF),
             pltpu.VMEM((n_samp, n_cent, pool, width), BF),
-            pltpu.VMEM((n_samp, n_cent, 1, block), F32),
+            pltpu.VMEM((n_samp, n_cent, 1, 2 * block), F32),
             pltpu.VMEM((slots, width), BF),
             pltpu.VMEM((slots, LANES), F32),
             pltpu.VMEM((slots, LANES), F32),
-            pltpu.VMEM((n_samp, 1, block), F32),
+            pltpu.VMEM((blocks, 1, block), F32),
             pltpu.VMEM((per_owner, width), F32),
-            pltpu.VMEM((n_samp, 1, block), F32),
-            dma((4,)),
+            pltpu.VMEM((n_cent, n_samp // 2, 1, 2 * block), F32),
+            dma((5,)),
             dma((n_samp, n_cent)), dma((n_samp, n_cent)), dma((n_samp, n_cent)), dma((n_samp, n_cent)),
             dma((n_cent,)), dma((n_cent,)), dma((n_samp,)), dma((n_samp,)),
             dma((n_samp, n_cent)), dma((n_samp, n_cent)),
+            dma((n_cent,)), dma((n_cent,)), dma((n_cent,)), dma((n_cent,)), dma((n_samp,)),
         ],
         compiler_params=pltpu.CompilerParams(collective_id=0, has_side_effects=True),
         name="dedup",
-    )(send, pooled, labels)
+    )(send, pooled, index, labels)
     keep = pl.pallas_call(
         pick_kernel,
         out_shape=shape((1, rows), F32),

time: 89.5 us -> 92.7 us (1.036)
  Pallas kernels: 85 us -> 88.2 us
    pallas_call x1, Pallas kernels: 78 us -> 81.3 us  [on_device(): pl.pallas_call(functools.partial(dedup_kernel, n_samp, n_cent), out_shape...]
where the time goes in v3:
time: 92.7 us; the launch traced here: 92.5 us
  Pallas kernels  88.2 us (95%)
  local copies, waits for them, and re-layouts  1.41 us (2%)
  other arithmetic  1.32 us (1%)
  between operations  1.31 us (1%)
    pallas_call x1, Pallas kernels, on_device(): pl.pallas_call(functools.partial(dedup_kernel, n_samp, n_cent), out_shape...  81.3 us
    pallas_call x1, Pallas kernels, on_device(): pl.pallas_call(functools.partial(pack_kernel, devices, n_cent, near, pool...  5.01 us
    pallas_call x1, Pallas kernels, on_device(): pl.pallas_call(pick_kernel, out_shape=shape((1, rows), F32), in_specs=[vm...  1.89 us

profile of v3, /device:TPU:0, one launch (start us, length us, event | category | flops | bytes accessed | tf_op | source)
XLA Modules:
  0.0 92.5 jit_solution(11178217470699239723)
XLA Ops:
  0.6 5.0 %pack.1 = (bf16[4,168,1024]{2,1,0:T(8,128)(2,1)}, bf16[32,1024]{1,0:T(8,128)(2,1)}, f32[4,1,256]{2,1,0:T(1,128)}, f32[32,1,512]{2,1,0:T(1,128)}, s32[8,512]{1,0:T(8,128)}) custom-call(f32[512,1024]{1,0:T(8,128)} %emb_ref.1, s32[1,512]{1,0:T(1,128)} %bitcast.62, s32[1,2048]{1,0:T(1,128)} %bitcast.51), custom_call_target="tpu_custom_call" | custom-call | tf_op jit(solution)/shard_map/pack/pallas_call | solution.py:492
  5.6 81.3 %dedup.1 = (f32[64,1024]{1,0:T(8,128)S(1)}, f32[64,1024]{1,0:T(8,128)S(1)}, f32[32,1,512]{2,1,0:T(1,128)}, f32[8,1,256]{2,1,0:T(1,128)}) custom-call(bf16[4,168,1024]{2,1,0:T(8,128)(2,1)} %get-tuple-element.137.send_ref, bf16[32,1024]{1,0:T(8,128)(2,1)} %get-tuple-element.138.pool_ref, f32[4,1,256]{2,1,0:T(1,128)} %get-tuple-element.139.index_ref, ...), custom_call_target="tpu_custom_call" | custom-call | tf_op jit(solution)/shard_map/dedup/pallas_call | solution.py:505
  86.9 1.3 %reduce_max.9 = f32[]{:T(128)} reduce(f32[8,1,256]{2,1,0:T(1,128)} %get-tuple-element.141, f32[]{:T(128)} %constant.72.clone.1), dimensions={0,1,2}, to_apply=%region_0.0 | reduce | flops 2047 | bytes 8200 | tf_op jit(solution)/shard_map/reduce_max | solution.py:551
  88.9 1.9 %pick.1 = f32[1,512]{1,0:T(1,128)S(1)} custom-call(f32[32,1,512]{2,1,0:T(1,128)} %get-tuple-element.142.back_ref, s32[8,512]{1,0:T(8,128)} %get-tuple-element.143.meta_ref), custom_call_target="tpu_custom_call" | custom-call | tf_op jit(solution)/shard_map/pick/pallas_call | solution.py:537
  90.8 0.2 conditional.1
  91.0 0.0 copy-start.1
  91.0 0.7 copy.38
  91.7 0.7 copy.39
  92.4 0.0 copy-done.1
Async XLA Ops:
  91.0 1.4 %copy-start.1 = (f32[512]{0:T(512)}, f32[512]{0:T(512)S(1)}, u32[]{:S(2)}) copy-start(f32[512]{0:T(512)S(1)} %get-tuple-element.272) | copy-start | bytes 6148

commit v4 on v3

--- a/solution.py
+++ b/solution.py
@@ -303,20 +303,27 @@
 
         score(p, load, tag)
 
+    order = []
+
+    def run(is_near, which):
+        order.append((is_near, which))
+        if is_near:
+            near_block(len(order) - 1, which)
+        else:
+            pool_block(len(order) - 1, which)
+
     for i in range(1, n_cent):
         c = (cent + i) % n_cent
         seat_copy(c, c).wait_recv()
         lane_copy(c, c).wait_recv()
         spread(c)
         pass_on(c)
-    order = [(True, 0)] + [(False, q) for q in range(quads // 2)]
-    order += [(True, i) for i in range(1, n_cent)]
-    order += [(False, q) for q in range(quads // 2, quads)]
-    for p, (is_near, which) in enumerate(order):
-        if is_near:
-            near_block(p, which)
-        else:
-            pool_block(p, which)
+        if i == 1:
+            run(True, 0)
+        for q in range((i - 1) * quads // (n_cent - 1), i * quads // (n_cent - 1)):
+            run(False, q)
+    for i in range(1, n_cent):
+        run(True, i)
 
     sums = sums_ref[...]
     scale = lax.rsqrt(jnp.sum(sums * sums, axis=1, keepdims=True) + EPSILON)

time: 92.7 us -> 88.7 us (0.957)
  Pallas kernels: 88.2 us -> 84.2 us
    pallas_call x1, Pallas kernels: 81.3 us -> 77.3 us  [on_device(): pl.pallas_call(functools.partial(dedup_kernel, n_samp, n_cent), out_shape...]
where the time goes in v4:
time: 88.7 us; the launch traced here: 88.4 us
  Pallas kernels  84.2 us (95%)
  local copies, waits for them, and re-layouts  1.41 us (2%)
  other arithmetic  1.32 us (1%)
  between operations  1.31 us (1%)
    pallas_call x1, Pallas kernels, on_device(): pl.pallas_call(functools.partial(dedup_kernel, n_samp, n_cent), out_shape...  77.3 us
    pallas_call x1, Pallas kernels, on_device(): pl.pallas_call(functools.partial(pack_kernel, devices, n_cent, near, pool...  5.01 us
    pallas_call x1, Pallas kernels, on_device(): pl.pallas_call(pick_kernel, out_shape=shape((1, rows), F32), in_specs=[vm...  1.89 us

profile of v4, /device:TPU:0, one launch (start us, length us, event | category | flops | bytes accessed | tf_op | source)
XLA Modules:
  0.0 88.4 jit_solution(15332535745920910454)
XLA Ops:
  0.6 5.0 %pack.1 = (bf16[4,168,1024]{2,1,0:T(8,128)(2,1)}, bf16[32,1024]{1,0:T(8,128)(2,1)}, f32[4,1,256]{2,1,0:T(1,128)}, f32[32,1,512]{2,1,0:T(1,128)}, s32[8,512]{1,0:T(8,128)}) custom-call(f32[512,1024]{1,0:T(8,128)} %emb_ref.1, s32[1,512]{1,0:T(1,128)} %bitcast.62, s32[1,2048]{1,0:T(1,128)} %bitcast.51), custom_call_target="tpu_custom_call" | custom-call | tf_op jit(solution)/shard_map/pack/pallas_call | solution.py:499
  5.6 77.3 %dedup.1 = (f32[64,1024]{1,0:T(8,128)S(1)}, f32[64,1024]{1,0:T(8,128)S(1)}, f32[32,1,512]{2,1,0:T(1,128)}, f32[8,1,256]{2,1,0:T(1,128)}) custom-call(bf16[4,168,1024]{2,1,0:T(8,128)(2,1)} %get-tuple-element.137.send_ref, bf16[32,1024]{1,0:T(8,128)(2,1)} %get-tuple-element.138.pool_ref, f32[4,1,256]{2,1,0:T(1,128)} %get-tuple-element.139.index_ref, ...), custom_call_target="tpu_custom_call" | custom-call | tf_op jit(solution)/shard_map/dedup/pallas_call | solution.py:512
  82.9 1.3 %reduce_max.9 = f32[]{:T(128)} reduce(f32[8,1,256]{2,1,0:T(1,128)} %get-tuple-element.141, f32[]{:T(128)} %constant.72.clone.1), dimensions={0,1,2}, to_apply=%region_0.0 | reduce | flops 2047 | bytes 8200 | tf_op jit(solution)/shard_map/reduce_max | solution.py:558
  84.9 1.9 %pick.1 = f32[1,512]{1,0:T(1,128)S(1)} custom-call(f32[32,1,512]{2,1,0:T(1,128)} %get-tuple-element.142.back_ref, s32[8,512]{1,0:T(8,128)} %get-tuple-element.143.meta_ref), custom_call_target="tpu_custom_call" | custom-call | tf_op jit(solution)/shard_map/pick/pallas_call | solution.py:544
  86.8 0.2 conditional.1
  87.0 0.0 copy-start.1
  87.0 0.7 copy.38
  87.7 0.7 copy.39
  88.4 0.0 copy-done.1
Async XLA Ops:
  87.0 1.4 %copy-start.1 = (f32[512]{0:T(512)}, f32[512]{0:T(512)S(1)}, u32[]{:S(2)}) copy-start(f32[512]{0:T(512)S(1)} %get-tuple-element.272) | copy-start | bytes 6148

commit v5 on v4

--- a/solution.py
+++ b/solution.py
@@ -384,7 +384,8 @@
         others(k, lambda c: back_copy(k, c, ((samp + k) % n_samp) * n_cent + c, c).wait_recv())
 
 
-def pick_kernel(back_ref, meta_ref, keep_ref):
+def pick_kernel(back_ref, meta_ref, tags_ref, keep_ref, top_ref):
+    top_ref[0, 0] = jnp.max(tags_ref[:, 0, :])
     devices = back_ref.shape[0]
     rows = meta_ref.shape[1]
     meta = meta_ref[...]
@@ -541,13 +542,14 @@
         compiler_params=pltpu.CompilerParams(collective_id=0, has_side_effects=True),
         name="dedup",
     )(send, pooled, index, labels)
-    keep = pl.pallas_call(
+    keep, top = pl.pallas_call(
         pick_kernel,
-        out_shape=shape((1, rows), F32),
-        in_specs=[vmem] * 2,
-        out_specs=vmem,
+        out_shape=(shape((1, rows), F32), shape((1, 1), F32)),
+        in_specs=[vmem] * 3,
+        out_specs=(vmem, pl.BlockSpec(memory_space=pltpu.SMEM)),
         name="pick",
-    )(back, meta).reshape(rows)
+    )(back, meta, tags)
+    keep = keep.reshape(rows)
 
     def fast(embeddings, assignment, owner_map, centroid, representative, keep):
         return centroid, representative, keep
@@ -555,7 +557,7 @@
     def slow(embeddings, assignment, owner_map, centroid, representative, keep):
         return full_capacity(embeddings, assignment, owner_map)
 
-    spilled = jnp.max(tags) >= SPILL
+    spilled = top[0, 0] >= SPILL
     return lax.cond(
         spilled, slow, fast, embeddings, assignment, owner_map, centroid, representative, keep
     )

time: 88.7 us -> 87.8 us (0.990)
  other arithmetic: 1.32 us -> 0 us
    reduce_max x1 -> x0, other arithmetic: 1.32 us -> none  [on_device(): spilled = jnp.max(tags) >= SPILL]
where the time goes in v5:
time: 87.8 us; the launch traced here: 87.6 us
  Pallas kernels  84.6 us (96%)
  local copies, waits for them, and re-layouts  1.41 us (2%)
  between operations  1.31 us (1%)
    pallas_call x1, Pallas kernels, on_device(): pl.pallas_call(functools.partial(dedup_kernel, n_samp, n_cent), out_shape...  77.3 us
    pallas_call x1, Pallas kernels, on_device(): pl.pallas_call(functools.partial(pack_kernel, devices, n_cent, near, pool...  5.01 us
    pallas_call x1, Pallas kernels, on_device(): pl.pallas_call(pick_kernel, out_shape=(shape((1, rows), F32), shape((1, 1...  2.36 us

profile of v5, /device:TPU:0, one launch (start us, length us, event | category | flops | bytes accessed | tf_op | source)
XLA Modules:
  0.0 87.6 jit_solution(14064151894602112946)
XLA Ops:
  0.6 5.0 %pack.1 = (bf16[4,168,1024]{2,1,0:T(8,128)(2,1)}, bf16[32,1024]{1,0:T(8,128)(2,1)}, f32[4,1,256]{2,1,0:T(1,128)}, f32[32,1,512]{2,1,0:T(1,128)}, s32[8,512]{1,0:T(8,128)}) custom-call(f32[512,1024]{1,0:T(8,128)} %emb_ref.1, s32[1,512]{1,0:T(1,128)} %bitcast.63, s32[1,2048]{1,0:T(1,128)} %bitcast.52), custom_call_target="tpu_custom_call" | custom-call | tf_op jit(solution)/shard_map/pack/pallas_call | solution.py:500
  5.6 77.3 %dedup.1 = (f32[64,1024]{1,0:T(8,128)S(1)}, f32[64,1024]{1,0:T(8,128)S(1)}, f32[32,1,512]{2,1,0:T(1,128)}, f32[8,1,256]{2,1,0:T(1,128)}) custom-call(bf16[4,168,1024]{2,1,0:T(8,128)(2,1)} %get-tuple-element.139.send_ref, bf16[32,1024]{1,0:T(8,128)(2,1)} %get-tuple-element.140.pool_ref, f32[4,1,256]{2,1,0:T(1,128)} %get-tuple-element.141.index_ref, ...), custom_call_target="tpu_custom_call" | custom-call | tf_op jit(solution)/shard_map/dedup/pallas_call | solution.py:513
  82.9 2.4 %pick.1 = (f32[1,512]{1,0:T(1,128)S(1)}, f32[1,1]{1,0:T(1,128)}) custom-call(f32[32,1,512]{2,1,0:T(1,128)} %get-tuple-element.143.back_ref, s32[8,512]{1,0:T(8,128)} %get-tuple-element.144.meta_ref, f32[8,1,256]{2,1,0:T(1,128)} %get-tuple-element.145.tags_ref), custom_call_target="tpu_custom_call" | custom-call | tf_op jit(solution)/shard_map/pick/pallas_call | solution.py:545
  85.9 0.2 conditional.1
  86.2 0.0 copy-start.1
  86.2 0.7 copy.38
  86.9 0.7 copy.39
  87.6 0.0 copy-done.1
Async XLA Ops:
  86.2 1.4 %copy-start.1 = (f32[512]{0:T(512)}, f32[512]{0:T(512)S(1)}, u32[]{:S(2)}) copy-start(f32[512]{0:T(512)S(1)} %get-tuple-element.276) | copy-start | bytes 6148
